TPU v7x, 32 devices: a whole 2x2x4 slice. The times are simulated.
32 devices in a mesh: ctx: 8 (over y, x, core), grp: 4 (over z).
Axes of the slice: x: 2, y: 2, z: 4, core: 2. Of those that a mesh axis runs over, the one named last changes fastest.
Arguments:
- query_in: bfloat16 [8192, 4096], P('ctx', 'grp'), may hold values from -6 to 6
- key_in: bfloat16 [8192, 4096], P('ctx', 'grp'), may hold values from -6 to 6
- value_in: bfloat16 [8192, 4096], P('ctx', 'grp'), may hold values from -6 to 6
- residues: float32 [256, 16], P('grp'), may hold values from -1.5 to 1.5
- decay_time: float32 [256, 16], P('grp'), may hold values from 20 to 32768
- skip_gain: float32 [4096], P('grp'), may hold values from 0.5 to 1.5
- out_proj: bfloat16 [4096, 4096], P('ctx', 'grp'), may hold values from -0.09375 to 0.09375
- doc_lengths: int32 [4], replicated, may hold values from 1 to 4096, 8192 in all
- grad_out: bfloat16 [8192, 4096], P('ctx', 'grp'), may hold values from -6 to 6
Outputs:
- mixed_out: bfloat16 [8192, 4096], P('ctx', 'grp')
- grad_query: bfloat16 [8192, 4096], P('ctx', 'grp')
- grad_key: bfloat16 [8192, 4096], P('ctx', 'grp')
- grad_value: bfloat16 [8192, 4096], P('ctx', 'grp')
- grad_proj: float32 [4096, 4096], P('ctx', 'grp')
Inputs may be any that keep to these rules, and one draw needn't show every extreme that they name: `doc_lengths`: document lengths in window order, summing to 8192; the longest is exactly 4096.
All inputs are finite; a program needn't handle non-finite values.
Results may differ from a plain program's by a relative error of at most 0.013.
Values may be sent and summed in bfloat16 or wider, within the bound.
A program may use at most 192 MiB of HBM per device.

v0:
```python
import jax
import jax.numpy as jnp
from jax import lax
from jax.sharding import PartitionSpec as P


def prefix(value, axis, combine, identity, reverse):
    size, position = (lax.axis_size(axis), lax.axis_index(axis))
    everything = jax.tree.map(
        lambda part, kind: lax.all_gather(part.astype(kind), axis),
        value,
        jax.tree.map(lambda a: jnp.bfloat16 if a.dtype == jnp.float32 else a.dtype, value),
    )
    start = jax.tree.map(
        lambda part, zero: jnp.broadcast_to(jnp.asarray(zero, part.dtype), part.shape),
        value,
        identity,
    )

    def step(k, before):
        at = size - 1 - k if reverse else k
        reached = at > position if reverse else at < position
        new = combine(
            before, jax.tree.map(lambda part, own: part[at].astype(own.dtype), everything, value)
        )
        return jax.tree.map(lambda a, b: jnp.where(reached, a, b), new, before)

    return lax.fori_loop(0, size, step, start)


def chain(former, latter):
    return (former[0] * latter[0], latter[0][:, None, :] * former[1] + latter[1])


def doc_index(starts, where_now):
    return jnp.sum((starts[None, :] <= where_now[:, None]).astype(jnp.int32), axis=1) - 1


def local(
    query_in, key_in, value_in, residues, decay_time, skip_gain, out_proj, doc_lengths, grad_out
):
    tok_rows, channels = query_in.shape
    filters, poles = residues.shape
    members = channels // filters
    block_len = min(128, tok_rows)
    block_count = tok_rows // block_len
    starts = jnp.cumsum(doc_lengths) - doc_lengths
    where_now = lax.axis_index("ctx") * tok_rows + jnp.arange(tok_rows, dtype=jnp.int32)
    doc_ids = doc_index(starts, where_now).reshape(block_count, block_len)
    prior_ids = doc_index(starts, where_now - 1).reshape(block_count, block_len)[:, 0]
    decay_rate = 1.0 / decay_time
    residue_scaled = residues * jnp.sqrt(-jnp.expm1(-2.0 * decay_rate))
    lag_steps = jnp.arange(block_len, dtype=jnp.float32)
    powers = jnp.exp(-lag_steps[None, None, :] * decay_rate[:, :, None])
    lagged = jnp.sum(residue_scaled[:, :, None] * powers, axis=1)
    positions = jnp.arange(block_len, dtype=jnp.int32)
    lag_index = jnp.clip(positions[:, None] - positions[None, :], 0, block_len - 1)
    toeplitz = jnp.take(lagged, lag_index, axis=1)
    causal = positions[:, None] >= positions[None, :]
    same_docs = (doc_ids[:, :, None] == doc_ids[:, None, :]) & causal[None]
    masked = toeplitz[None] * same_docs[:, None].astype(jnp.float32)
    step_enter = jnp.exp(-(lag_steps + 1.0)[None, None, :] * decay_rate[:, :, None])
    alive_enter = (doc_ids == prior_ids[:, None]).astype(jnp.float32)
    enter_gain = residue_scaled[None, :, :, None] * step_enter[None] * alive_enter[:, None, None, :]
    step_leave = jnp.exp(-(block_len - 1.0 - lag_steps)[None, None, :] * decay_rate[:, :, None])
    alive_leave = (doc_ids == doc_ids[:, -1:]).astype(jnp.float32)
    leave_gain = step_leave[None] * alive_leave[:, None, None, :]
    across_gain = (
        jnp.exp(-block_len * decay_rate)[None]
        * (prior_ids == doc_ids[:, -1]).astype(jnp.float32)[:, None, None]
    )
    unit_decay = jnp.ones((filters, poles), jnp.float32)
    empty_state = jnp.zeros((filters, members, poles), jnp.float32)
    highest = lax.Precision.HIGHEST
    query_f = query_in.astype(jnp.float32)
    key_f = key_in.astype(jnp.float32)
    value_f = value_in.astype(jnp.float32)
    product_f = (key_f * value_f).astype(jnp.bfloat16).astype(jnp.float32)
    gathered = lax.all_gather(out_proj, "ctx", axis=0, tiled=True)
    shaped = product_f.reshape(block_count, block_len, filters, members)
    within = jnp.einsum("bgts,bsgc->btgc", masked, shaped, precision=highest)
    block_state = jnp.einsum("bgns,bsgc->bgcn", leave_gain, shaped, precision=highest)
    summary = (unit_decay, empty_state)
    for number in range(block_count):
        summary = chain(summary, (across_gain[number], block_state[number]))
    incoming = prefix(summary, "ctx", chain, (unit_decay, empty_state), False)[1]
    entering = []
    for number in range(block_count):
        entering.append(incoming)
        incoming = across_gain[number][:, None, :] * incoming + block_state[number]
    beyond = jnp.einsum("bgnt,bgcn->btgc", enter_gain, jnp.stack(entering), precision=highest)
    convolved = (within + beyond).reshape(tok_rows, channels)
    grad_full = lax.all_gather(grad_out, "grp", axis=1, tiled=True)
    grad_gated = jnp.dot(grad_full, gathered, preferred_element_type=jnp.float32)
    grad_filtered = grad_gated * query_f
    shaped = grad_filtered.reshape(block_count, block_len, filters, members)
    within = jnp.einsum("bgts,btgc->bsgc", masked, shaped, precision=highest)
    block_adjoint = jnp.einsum("bgnt,btgc->bgcn", enter_gain, shaped, precision=highest)
    summary = (unit_decay, empty_state)
    for number in reversed(range(block_count)):
        summary = chain(summary, (across_gain[number], block_adjoint[number]))
    incoming = prefix(summary, "ctx", chain, (unit_decay, empty_state), True)[1]
    leaving = [None] * block_count
    for number in reversed(range(block_count)):
        leaving[number] = incoming
        incoming = block_adjoint[number] + across_gain[number][:, None, :] * incoming
    beyond = jnp.einsum("bgns,bgcn->bsgc", leave_gain, jnp.stack(leaving), precision=highest)
    grad_product = (within + beyond).reshape(tok_rows, channels) + skip_gain * grad_filtered
    grad_full, grad_gated, grad_product = (grad_full, grad_gated, grad_product)
    filtered = convolved + skip_gain * product_f
    gated = (query_f * filtered).astype(jnp.bfloat16)
    partial_value = lax.dot_general(
        gated, gathered, (((1,), (1,)), ((), ())), preferred_element_type=jnp.float32
    )
    rounded = lax.optimization_barrier(partial_value.astype(jnp.bfloat16)).astype(jnp.float32)
    mixed_out = lax.psum_scatter(
        rounded.astype(jnp.bfloat16), "grp", scatter_dimension=1, tiled=True
    )
    grad_query = (grad_gated * filtered).astype(jnp.bfloat16)
    grad_key = (grad_product * value_f).astype(jnp.bfloat16)
    grad_value = (grad_product * key_f).astype(jnp.bfloat16)
    term_whole = lax.dot_general(
        grad_full, gated, (((0,), (0,)), ((), ())), preferred_element_type=jnp.float32
    )
    grad_proj = lax.psum_scatter(
        term_whole.astype(jnp.bfloat16), "ctx", scatter_dimension=0, tiled=True
    ).astype(jnp.float32)
    return (mixed_out, grad_query, grad_key, grad_value, grad_proj)


def solution(mesh):
    return jax.shard_map(
        local,
        mesh=mesh,
        in_specs=(
            P("ctx", "grp"),
            P("ctx", "grp"),
            P("ctx", "grp"),
            P("grp", None),
            P("grp", None),
            P("grp"),
            P("ctx", "grp"),
            P(),
            P("ctx", "grp"),
        ),
        out_specs=(
            P("ctx", "grp"),
            P("ctx", "grp"),
            P("ctx", "grp"),
            P("ctx", "grp"),
            P("ctx", "grp"),
        ),
        check_vma=False,
    )
```

profile of v0, /device:TPU:0, one launch (start us, length us, event | category | flops | bytes accessed | tf_op | source)
XLA Modules:
  0.0 472.9 jit_solution(16849011690872754440)
XLA Ops:
  11.7 3.9 fusion.20
  15.6 3.9 copy.180
  26.9 3.4 fusion.16
  35.3 10.7 %all_gather.22 = bf16[8,64,16]{1,2,0:T(8,128)(2,1)S(1)} all-gather(bf16[1,64,16]{1,2,0:T(8,128)(2,1)} %get-tuple-element.365), channel_id=1, replica_groups=mesh['ctx'=8,'grp'=4] {'ctx'}, dimensions={0}, use_global_device_ids=true | all-gather | bytes 18432 | tf_op jit(solution)/shard_map/all_gather | solution.py:10
  46.0 10.2 %all_gather.23 = bf16[8,64,16,16]{1,3,2,0:T(8,128)(2,1)S(1)} all-gather(bf16[1,64,16,16]{1,3,2,0:T(8,128)(2,1)} %copy.195), channel_id=1, replica_groups=mesh['ctx'=8,'grp'=4] {'ctx'}, dimensions={0}, use_global_device_ids=true | all-gather | bytes 294912 | tf_op jit(solution)/shard_map/all_gather | solution.py:10
  58.9 54.4 %gather_fusion = f32[16384,64]{1,0:T(8,128)} fusion(f32[64,128]{0,1:T(8,128)S(1)} %copy.183, s32[16384]{0:T(1024)S(1)} %fusion.41), kind=kCustom, calls=%fused_computation | custom fusion | bytes 8454144 | tf_op jit(solution)/shard_map/jit(_take)/gather | solution.py:58
  113.3 10.0 %select_bitcast_fusion = f32[64,128,128]{0,2,1:T(8,128)} fusion(f32[128,128,64]{2,1,0:T(8,128)} %bitcast.199, pred[128,128]{1,0:T(8,128)(4,1)S(1)} %fusion.44), kind=kLoop, calls=%fused_computation.15 | loop fusion | flops 1048576 | bytes 8404992 | tf_op jit(solution)/shard_map/jit(_take)/select_n | solution.py:58
  123.3 7.3 %copy.184 = f32[64,128,128]{2,1,0:T(8,128)} copy(f32[64,128,128]{0,2,1:T(8,128)} %select_bitcast_fusion) | data formatting | bytes 8388608 | tf_op jit(solution)/shard_map/jit(_take)/select_n | solution.py:58
  134.4 5.2 %fusion.12 = f32[8,64,16,128]{3,2,1,0:T(8,128)S(1)} fusion(f32[8,64,16,16]{3,2,1,0:T(8,128)S(1)} %bitcast_dynamic-update-slice_fusion.8, f32[8,128]{1,0:T(8,128)S(1)} %get-tuple-element.379, f32[64,16,128]{2,1,0:T(8,128)S(1)} %get-tuple-element.369), kind=kOutput, calls=%fused_computation.20 | convolution fusion | flops 202375168 | bytes 5246976 | tf_op jit(solution)/shard_map/bgnt,bgcn->btgc/dot_general | solution.py:91
  139.6 26.8 %add_bitcast_fusion.1 = f32[8,128,64,16]{1,3,2,0:T(8,128)S(1)} fusion(f32[8,64,16,128]{3,2,1,0:T(8,128)S(1)} %fusion.12, f32[8,128,128]{2,1,0:T(8,128)S(1)} %and_convert_fusion, f32[64,128,128]{2,1,0:T(8,128)S(1)} %copy-done, bf16[8,128,64,16]{1,0,3,2:T(8,128)(2,1)S(1)} %bitcast.198), kind=kOutput, calls=%fused_computation.41 | convolution fusion | flops 1620049920 | bytes 15204352 | tf_op jit(solution)/shard_map/bgts,bsgc->btgc/dot_general | solution.py:81
  171.8 5.5 %copy.206 = f32[1024,1024]{1,0:T(8,128)} copy(f32[1024,1024]{0,1:T(8,128)} %bitcast.201) | data formatting | bytes 8388608 | tf_op jit(solution)/shard_map/reshape | solution.py:92
  177.3 39.1 %all-gather.3.cloned.1.call-done = bf16[4096,1024]{1,0:T(8,128)(2,1)} async-done(((bf16[512,1024]{1,0:T(8,128)(2,1)}), bf16[4096,1024]{1,0:T(8,128)(2,1)}) %all-gather.3.cloned.1.call-update) | async-done | bytes 8388624 | tf_op jit(solution)/shard_map/all_gather | solution.py:79
  216.5 17.5 %multiply_convert_fusion = (bf16[1024,1024]{1,0:T(8,128)(2,1)}, bf16[1024,1024]{1,0:T(8,128)(2,1)S(1)}, f32[1024,1024]{1,0:T(8,128)}) fusion(f32[1024,1024]{1,0:T(8,128)} %copy.206, bf16[1024,1024]{1,0:T(8,128)(2,1)S(1)} %copy-done.9, f32[1024]{0:T(1024)S(1)} %copy-done.17, bf16[1024,1024]{1,0:T(8,128)(2,1)} %param.13, ...), kind=kOutput, calls=%fused_computation.39 | convolution fusion | flops 8599371776 | bytes 33558528 | tf_op jit(solution)/shard_map/dot_general | solution.py:94
  235.2 11.4 %convert_bitcast_fusion = bf16[4096,1024]{0,1:T(8,128)(2,1)} fusion(bf16[1024,1024]{1,0:T(8,128)(2,1)S(1)} %get-tuple-element.359, bf16[1024,4096]{1,0:T(8,128)(2,1)S(1)} %copy-done.18), kind=kOutput, calls=%fused_computation.16 | convolution fusion | flops 8594128896 | bytes 18874368 | tf_op jit(solution)/shard_map/dot_general | solution.py:122
  248.2 14.5 %convolution_convert_fusion = bf16[1024,4096]{1,0:T(8,128)(2,1)} fusion(bf16[1024,1024]{1,0:T(8,128)(2,1)S(1)} %copy-done.21, bf16[4096,1024]{1,0:T(8,128)(2,1)} %all-gather.3.cloned.1.call-done), kind=kOutput, calls=%fused_computation.17 | convolution fusion | flops 8594128896 | bytes 18874368 | tf_op jit(solution)/shard_map/dot_general | solution.py:112
  263.5 9.0 %all_gather.26 = bf16[8,64,16]{1,2,0:T(8,128)(2,1)S(1)} all-gather(bf16[1,64,16]{1,2,0:T(8,128)(2,1)S(1)} %get-tuple-element.363), channel_id=1, replica_groups=mesh['ctx'=8,'grp'=4] {'ctx'}, dimensions={0}, use_global_device_ids=true | all-gather | bytes 18432 | tf_op jit(solution)/shard_map/all_gather | solution.py:10
  272.5 5.3 %copy.207 = f32[1024,1024]{0,1:T(8,128)} copy(f32[1024,1024]{1,0:T(8,128)} %get-tuple-element.360) | data formatting | bytes 8388608 | tf_op jit(solution)/shard_map/mul | solution.py:95
  281.2 7.0 %fusion.10 = f32[8,64,16,16]{3,2,1,0:T(8,128)S(1)} fusion(f32[8,128,64,16]{1,0,3,2:T(8,128)S(1)} %bitcast.195, f32[8,128]{1,0:T(8,128)S(1)} %get-tuple-element.379, f32[64,16,128]{2,1,0:T(8,128)S(1)} %get-tuple-element.369), kind=kOutput, calls=%fused_computation.18 | convolution fusion | flops 202375168 | bytes 5246976 | tf_op jit(solution)/shard_map/bgnt,btgc->bgcn/dot_general | solution.py:98
  290.9 10.2 %all_gather.27 = bf16[8,64,16,16]{1,3,2,0:T(8,128)(2,1)S(1)} all-gather(bf16[1,64,16,16]{1,3,2,0:T(8,128)(2,1)S(1)} %copy.213), channel_id=1, replica_groups=mesh['ctx'=8,'grp'=4] {'ctx'}, dimensions={0}, use_global_device_ids=true | all-gather | bytes 294912 | tf_op jit(solution)/shard_map/all_gather | solution.py:10
  309.4 29.0 %fusion.2 = f32[8,64,16,128]{3,2,1,0:T(8,128)S(1)} fusion(f32[8,128,128]{2,1,0:T(8,128)S(1)} %copy-done.11, f32[64,128,128]{2,1,0:T(8,128)S(1)} %copy-done.1, f32[8,128,64,16]{1,0,3,2:T(8,128)S(1)} %bitcast.196), kind=kOutput, calls=%fused_computation.7 | convolution fusion | flops 1619001344 | bytes 13107200 | tf_op jit(solution)/shard_map/bgts,btgc->bsgc/dot_general | solution.py:97
  338.4 5.0 %add_bitcast_fusion = f32[8,128,64,16]{1,3,2,0:T(8,128)S(1)} fusion(f32[8,64,16,128]{3,2,1,0:T(8,128)S(1)} %fusion.2, f32[8,64,16,16]{3,2,1,0:T(8,128)S(1)} %bitcast_dynamic-update-slice_fusion, f32[8,128]{1,0:T(8,128)S(1)} %get-tuple-element.380, f32[64,16,128]{2,1,0:T(8,128)S(1)} %copy-done.13), kind=kOutput, calls=%fused_computation.38 | convolution fusion | flops 203423744 | bytes 9441280 | tf_op jit(solution)/shard_map/bgns,bgcn->bsgc/dot_general | solution.py:107
  348.8 5.5 %copy.217 = f32[1024,1024]{1,0:T(8,128)} copy(f32[1024,1024]{0,1:T(8,128)} %bitcast.203) | data formatting | bytes 8388608 | tf_op jit(solution)/shard_map/reshape | solution.py:108
  354.3 7.8 %fusion.19 = (bf16[1024,1024]{1,0:T(8,128)(2,1)}, bf16[1024,1024]{1,0:T(8,128)(2,1)}) fusion(bf16[1024,1024]{1,0:T(8,128)(2,1)} %param.14, f32[1024,1024]{1,0:T(8,128)} %copy.217, f32[1024,1024]{1,0:T(8,128)} %get-tuple-element.360, f32[1024]{0:T(1024)S(1)} %copy-done.17, bf16[1024,1024]{1,0:T(8,128)(2,1)S(1)} %copy-done.8), kind=kLoop, calls=%fused_computation.32 | loop fusion | flops 8388608 | bytes 16781312 | tf_op jit(solution)/shard_map/convert_element_type | solution.py:121
  364.7 101.5 %reduce-scatter.3.cloned.1.call-done = bf16[1024,1024]{1,0:T(8,128)(2,1)} async-done(((bf16[1024,4096]{1,0:T(8,128)(2,1)}), bf16[1024,1024]{1,0:T(8,128)(2,1)}) %reduce-scatter.3.cloned.1.call-update) | async-done | bytes 2097168 | tf_op jit(solution)/shard_map/reduce_scatter | solution.py:116
  (154 shorter events, 55.6 us)
Async XLA Ops:
  7.2 4.5 copy-start.7
  7.2 170.2 %all-gather.5.cloned.1.call-start = ((), (), s32[]{:S(2)}) async-start(), calls=%async_computation.4 | async-start | bytes 10485760 | tf_op jit(solution)/shard_map/all_gather | solution.py:93
  7.9 208.5 %all-gather.3.cloned.1.call-start = ((), (), s32[]{:S(2)}) async-start(), calls=%async_computation.2 | async-start | bytes 9437184 | tf_op jit(solution)/shard_map/all_gather | solution.py:79
  8.7 353.4 %reduce-scatter.5.cloned.1.call-start = ((), (), s32[]{:S(2)}) async-start(), calls=%async_computation.5 | async-start | bytes 9437184 | tf_op jit(solution)/shard_map/reduce_scatter | solution.py:125
  15.6 6.5 %copy-start.19 = (s32[4]{0:T(128)S(1)}, s32[4]{0:T(128)}, u32[]{:S(2)}) copy-start(s32[4]{0:T(128)} %param.20) | copy-start | bytes 52
  25.0 8.5 %copy-start.14 = (f32[64,16]{1,0:T(8,128)}, f32[64,16]{1,0:T(8,128)S(1)}, u32[]{:S(2)}) copy-start(f32[64,16]{1,0:T(8,128)S(1)} %copy.186) | copy-start | bytes 12292
  26.9 6.6 %copy-start.12 = (f32[64,16,128]{2,1,0:T(8,128)}, f32[64,16,128]{2,1,0:T(8,128)S(1)}, u32[]{:S(2)}) copy-start(f32[64,16,128]{2,1,0:T(8,128)S(1)} %get-tuple-element.375) | copy-start | bytes 1572868
  30.3 2.1 copy-start.3
  130.6 3.1 copy-start.4
  130.9 8.7 %copy-start.10 = (f32[8,128,128]{2,1,0:T(8,128)}, f32[8,128,128]{2,1,0:T(8,128)S(1)}, u32[]{:S(2)}) copy-start(f32[8,128,128]{2,1,0:T(8,128)S(1)} %and_convert_fusion) | copy-start | bytes 1572868
  134.4 5.2 %copy-start = (f32[64,128,128]{2,1,0:T(8,128)S(1)}, f32[64,128,128]{2,1,0:T(8,128)}, u32[]{:S(2)}) copy-start(f32[64,128,128]{2,1,0:T(8,128)} %copy.184) | copy-start | bytes 12582916
  171.8 44.6 %copy-start.9 = (bf16[1024,1024]{1,0:T(8,128)(2,1)S(1)}, bf16[1024,1024]{1,0:T(8,128)(2,1)}, u32[]{:S(2)}) copy-start(bf16[1024,1024]{1,0:T(8,128)(2,1)} %fusion.20) | copy-start | bytes 6291460
  171.8 44.6 %copy-start.17 = (f32[1024]{0:T(1024)S(1)}, f32[1024]{0:T(1024)}, u32[]{:S(2)}) copy-start(f32[1024]{0:T(1024)} %param.18) | copy-start | bytes 12292
  216.5 18.8 %copy-start.18 = (bf16[1024,4096]{1,0:T(8,128)(2,1)S(1)}, bf16[1024,4096]{1,0:T(8,128)(2,1)}, u32[]{:S(2)}) copy-start(bf16[1024,4096]{1,0:T(8,128)(2,1)} %all-gather.5.cloned.1.call-done) | copy-start | bytes 25165828
  246.6 1.6 copy-start.21
  246.6 219.5 %reduce-scatter.3.cloned.1.call-start = ((), (), s32[]{:S(2)}) async-start(), calls=%async_computation.3 | async-start | bytes 10485760 | tf_op jit(solution)/shard_map/reduce_scatter | solution.py:116
  281.2 7.0 %copy-start.5 = (f32[128,8,8,128]{3,2,1,0:T(8,128)}, f32[128,8,8,128]{3,2,1,0:T(8,128)S(1)}, u32[]{:S(2)}) copy-start(f32[128,8,8,128]{3,2,1,0:T(8,128)S(1)} %copy.221) | copy-start | bytes 12582916
  288.2 2.0 copy-start.2
  290.3 11.9 %copy-start.15 = (f32[64,16]{1,0:T(8,128)S(1)}, f32[64,16]{1,0:T(8,128)}, u32[]{:S(2)}) copy-start(f32[64,16]{1,0:T(8,128)} %copy-done.14) | copy-start | bytes 12292
  304.9 4.5 copy-start.1
  304.9 4.5 copy-start.6
  304.9 4.5 copy-start.11
  309.4 29.0 %copy-start.13 = (f32[64,16,128]{2,1,0:T(8,128)S(1)}, f32[64,16,128]{2,1,0:T(8,128)}, u32[]{:S(2)}) copy-start(f32[64,16,128]{2,1,0:T(8,128)} %copy-done.12) | copy-start | bytes 1572868
  348.8 5.5 %copy-start.8 = (bf16[1024,1024]{1,0:T(8,128)(2,1)S(1)}, bf16[1024,1024]{1,0:T(8,128)(2,1)}, u32[]{:S(2)}) copy-start(bf16[1024,1024]{1,0:T(8,128)(2,1)} %param.15) | copy-start | bytes 6291460
  (2 other events, 2.0 us)
Sparse Core Ops, SparseCore 0:
  9.6 152.3 all-gather.4
  163.8 52.5 all-gather.2
  246.8 71.9 reduce-scatter.4
  321.7 144.4 reduce-scatter.2
where the time goes:
time: 480 us; the launch traced here: 473 us
  waiting for transfers between devices  142 us (30%)
  matrix products  120 us (25%)
  local copies, waits for them, and re-layouts  116 us (24%)
  blocking collectives  40 us (8%)
  other arithmetic  39.7 us (8%)
  between operations  14.4 us (3%)
    reduce_scatter x1, waiting for transfers between devices, local(): lax.psum_scatter(rounded.astype(jnp.bfloat16), 'grp', scatter_dimension=1...  102 us
    gather x1, local copies, waits for them, and re-layouts, local(): toeplitz = jnp.take(lagged, lag_index, axis=1)  54.4 us
    all_gather x4, blocking collectives, prefix(): lax.all_gather(part.astype(kind), axis)  40 us
    all_gather x1, waiting for transfers between devices, local(): gathered = lax.all_gather(out_proj, 'ctx', axis=0, tiled=True)  39.1 us
    dot_general x1, matrix products, local(): within = jnp.einsum('bgts,btgc->bsgc', masked, shaped, precision=highest)  29 us
    dot_general x1, matrix products, local(): within = jnp.einsum('bgts,bsgc->btgc', masked, shaped, precision=highest)  26.8 us
    unnamed x53, local copies, waits for them, and re-layouts  22.2 us
    dot_general x1, matrix products, local(): jnp.dot(grad_full, gathered, preferred_element_type=jnp.float32)  17.5 us
  transfers between devices with their start and end apart: 4, of which 2 were waited for; matrix products, arithmetic and copies ran while one was open for 51% of the time, Pallas kernels for 0%

commit v1 on v0

v1 whole, which is shorter than its diff:
```python
import functools

import jax
import jax.numpy as jnp
from jax import lax
from jax.experimental import pallas as pl
from jax.experimental.pallas import tpu as pltpu
from jax.sharding import PartitionSpec as P

LANES = 128
BLOCK = 128
F32 = jnp.float32
BF16 = jnp.bfloat16


def doc_index(starts, where_now):
    return jnp.sum((starts[None, :] <= where_now[:, None]).astype(jnp.int32), axis=1) - 1


def pick(stacked, count, rows, members):
    lane_filter = lax.broadcasted_iota(jnp.int32, (rows, LANES), 1) // members
    out = stacked[:rows]
    for g in range(1, count):
        out = jnp.where(lane_filter == g, stacked[g * rows:(g + 1) * rows], out)
    return out


def summary_kernel(count, poles, members, a_ref, b_ref, leave_ref, out_ref):
    line = (a_ref[...].astype(F32) * b_ref[...].astype(F32)).astype(BF16)
    stacked = jnp.dot(leave_ref[...], line, preferred_element_type=F32)
    out_ref[...] = pick(stacked, count, poles, members).astype(out_ref.dtype)


def summarize(a, b, leave, poles, members):
    rows, channels = a.shape
    count = LANES // members
    return pl.pallas_call(
        functools.partial(summary_kernel, count, poles, members),
        grid=(channels // LANES,),
        in_specs=[
            pl.BlockSpec((rows, LANES), lambda j: (0, j)),
            pl.BlockSpec((rows, LANES), lambda j: (0, j)),
            pl.BlockSpec((count * poles, rows), lambda j: (j, 0)),
        ],
        out_specs=pl.BlockSpec((poles, LANES), lambda j: (0, j)),
        out_shape=jax.ShapeDtypeStruct((poles, channels), BF16),
        cost_estimate=pl.CostEstimate(
            flops=2 * rows * channels * poles * count,
            bytes_accessed=rows * channels * 8,
            transcendentals=0,
        ),
    )(a, b, leave)


def convolve(reverse, count, poles, members, blocks, line_of, emit, lag_ref, gain_ref, mask_ref,
             leave_ref, alive_ref, across_ref, alive_across_ref, enter_ref, base):
    for g in range(count):
        row = jnp.broadcast_to(lag_ref[g:g + 1, :], (BLOCK, LANES))
        matrix = pltpu.roll(row, 0, 1, stride=1, stride_axis=0)
        base[g * BLOCK:(g + 1) * BLOCK, :LANES] = matrix.astype(BF16)
    base[:, LANES:] = gain_ref[...]
    state = enter_ref[...]
    for step in range(blocks):
        b = blocks - 1 - step if reverse else step
        line = line_of(b)
        low = line.astype(BF16)
        mask = mask_ref[b]
        left = (base[...].reshape(count, BLOCK, LANES + poles) * mask[None]).reshape(
            count * BLOCK, LANES + poles
        )
        right = jnp.concatenate([low, state.astype(BF16)], axis=0)
        result = pick(
            jnp.dot(left, right, preferred_element_type=F32), count, BLOCK, members
        )
        emit(b, line, result)
        if step < blocks - 1:
            gone = leave_ref[...] * alive_ref[b:b + 1, :]
            fresh = pick(
                jnp.dot(gone.astype(BF16), low, preferred_element_type=F32), count, poles, members
            )
            state = across_ref[...] * alive_across_ref[b:b + 1, :] * state + fresh


def forward_kernel(count, poles, members, blocks, query, key, value, skip, lag, gain, mask, leave,
                   alive, across, alive_across, enter, filtered, gated, base):
    def rows(b):
        return pl.ds(b * BLOCK, BLOCK)

    def line_of(b):
        return (key[rows(b), :].astype(F32) * value[rows(b), :].astype(F32)).astype(BF16).astype(F32)

    def emit(b, line, result):
        result = result + skip[...] * line
        filtered[rows(b), :] = result
        gated[rows(b), :] = (query[rows(b), :].astype(F32) * result).astype(BF16)

    convolve(False, count, poles, members, blocks, line_of, emit, lag, gain, mask, leave, alive,
             across, alive_across, enter, base)


def backward_kernel(count, poles, members, blocks, query, key, value, grad_gated, filtered, skip,
                    lag, gain, mask, leave, alive, across, alive_across, enter, grad_query,
                    grad_key, grad_value, base):
    def rows(b):
        return pl.ds(b * BLOCK, BLOCK)

    def line_of(b):
        grad = grad_gated[rows(b), :]
        grad_query[rows(b), :] = (grad * filtered[rows(b), :]).astype(BF16)
        return grad * query[rows(b), :].astype(F32)

    def emit(b, line, result):
        result = result + skip[...] * line
        grad_key[rows(b), :] = (result * value[rows(b), :].astype(F32)).astype(BF16)
        grad_value[rows(b), :] = (result * key[rows(b), :].astype(F32)).astype(BF16)

    convolve(True, count, poles, members, blocks, line_of, emit, lag, gain, mask, leave, alive,
             across, alive_across, enter, base)


def run_conv(kernel, wide, skip, tables, enter, out_types, poles, members):
    rows, channels = wide[0].shape
    count = LANES // members
    blocks = rows // BLOCK
    column = pl.BlockSpec((rows, LANES), lambda j: (0, j))
    lag, gain, mask, leave, alive, across, alive_across = tables
    return pl.pallas_call(
        functools.partial(kernel, count, poles, members, blocks),
        grid=(channels // LANES,),
        in_specs=[column] * len(wide) + [
            pl.BlockSpec((1, LANES), lambda j: (0, j)),
            pl.BlockSpec((count, BLOCK), lambda j: (j, 0)),
            pl.BlockSpec((count * BLOCK, poles), lambda j: (j, 0)),
            pl.BlockSpec((blocks, BLOCK, BLOCK + poles), lambda j: (0, 0, 0)),
            pl.BlockSpec((count * poles, BLOCK), lambda j: (j, 0)),
            pl.BlockSpec((blocks, BLOCK), lambda j: (0, 0)),
            pl.BlockSpec((poles, LANES), lambda j: (0, j)),
            pl.BlockSpec((blocks, LANES), lambda j: (0, 0)),
            pl.BlockSpec((poles, LANES), lambda j: (0, j)),
        ],
        out_specs=[column] * len(out_types),
        out_shape=[jax.ShapeDtypeStruct((rows, channels), kind) for kind in out_types],
        scratch_shapes=[pltpu.VMEM((count * BLOCK, BLOCK + poles), BF16)],
        cost_estimate=pl.CostEstimate(
            flops=16 * rows * channels * BLOCK * 2, bytes_accessed=rows * channels * 14, transcendentals=0
        ),
    )(*wide, skip, lag, gain, mask, leave, alive, across, alive_across, enter)


def swap(value, flip, size):
    return lax.ppermute(value, "ctx", [(i, i ^ flip) for i in range(size)])


def gather_rows(own, size, me):
    if size != 8:
        return lax.all_gather(own, "ctx", axis=0, tiled=True)
    half = own.shape[0] // 2
    by_x, by_y = swap(own, 2, size), swap(own, 4, size)
    first, second = swap(by_x[:half], 4, size), swap(by_y[half:], 2, size)
    parts = {0: [own], 2: [by_x], 4: [by_y], 6: [first, second]}
    for flip in (0, 2, 4, 6):
        parts[flip ^ 1] = [swap(part, 1, size) for part in parts[flip]]
    rows, columns = own.shape
    whole = jnp.zeros((rows * size, columns), own.dtype)
    for flip, pieces in parts.items():
        at = (me ^ flip) * rows
        for piece in pieces:
            whole = lax.dynamic_update_slice(whole, piece, (at, 0))
            at = at + piece.shape[0]
    return whole


def scatter_terms(grad_full, gated, size, me):
    contract = (((0,), (0,)), ((), ()))
    if size != 8:
        term = lax.dot_general(grad_full, gated, contract, preferred_element_type=F32).astype(BF16)
        return term, lambda term: lax.psum_scatter(term, "ctx", scatter_dimension=0, tiled=True).astype(F32)
    width = grad_full.shape[1] // size

    def chunk(flip):
        part = lax.dynamic_slice_in_dim(grad_full, (me ^ flip) * width, width, axis=1)
        return lax.dot_general(part, gated, contract, preferred_element_type=F32).astype(BF16)

    terms = {flip: chunk(flip) for flip in (7, 3, 5, 1, 6, 2, 4, 0)}

    def finish(terms):
        half = gated.shape[1] // 2
        sums = {}
        for flip in (6, 2, 4, 0):
            sums[flip] = terms[flip].astype(F32) + swap(terms[flip ^ 1], 1, size).astype(F32)

        def route(columns, near, far):
            far_sum = sums[far][:, columns] + swap(sums[6][:, columns].astype(BF16), near, size).astype(F32)
            own_sum = sums[0][:, columns] + swap(sums[near][:, columns].astype(BF16), near, size).astype(F32)
            return own_sum + swap(far_sum.astype(BF16), far, size).astype(F32)

        return jnp.concatenate([route(slice(0, half), 2, 4), route(slice(half, None), 4, 2)], axis=1)

    return terms, finish


def local(
    query_in, key_in, value_in, residues, decay_time, skip_gain, out_proj, doc_lengths, grad_out
):
    rows, channels = query_in.shape
    filters, poles = residues.shape
    members = channels // filters
    blocks = rows // BLOCK
    size, me = lax.axis_size("ctx"), lax.axis_index("ctx")
    gathered = gather_rows(out_proj, size, me)
    grad_full = lax.all_gather(grad_out, "grp", axis=1, tiled=True)

    starts = jnp.cumsum(doc_lengths) - doc_lengths
    flat_ids = doc_index(starts, me * rows + jnp.arange(rows, dtype=jnp.int32))
    ids = flat_ids.reshape(blocks, BLOCK)
    firsts, lasts = ids[:, 0], ids[:, -1]
    before = doc_index(starts, me * rows - 1 + BLOCK * jnp.arange(blocks + 1, dtype=jnp.int32))
    after = doc_index(starts, me * rows + BLOCK * jnp.arange(1, blocks + 1, dtype=jnp.int32))
    ends = doc_index(starts, rows * jnp.arange(1, size + 1, dtype=jnp.int32) - 1)
    opens = doc_index(starts, rows * jnp.arange(size, dtype=jnp.int32))
    rate = 1.0 / decay_time
    beta = residues * jnp.sqrt(-jnp.expm1(-2.0 * rate))
    lags = jnp.arange(BLOCK, dtype=F32)
    rate_chan = jnp.repeat(rate.T, members, axis=1)
    response = jnp.sum(beta[:, :, None] * jnp.exp(-lags[None, None, :] * rate[:, :, None]), axis=1)
    mirrored = jnp.concatenate([response[:, :1], response[:, :0:-1]], axis=1)
    gain = beta[:, None, :] * jnp.exp(-(lags + 1.0)[None, :, None] * rate[:, None, :])
    gain_rev = gain[:, ::-1, :]
    leave_rev = jnp.exp(-lags[None, :] * rate.reshape(-1, 1))
    leave = jnp.exp(-(BLOCK - 1.0 - lags)[None, :] * rate.reshape(-1, 1))
    across = jnp.exp(-BLOCK * rate_chan)
    same = ids[:, :, None] == ids[:, None, :]
    place = jnp.arange(BLOCK)
    causal = place[:, None] >= place[None, :]

    def mask_of(order, alive):
        tail = jnp.broadcast_to(alive[:, :, None], (blocks, BLOCK, poles))
        return jnp.concatenate([same & order[None], tail], axis=2).astype(BF16)

    def spread(flags):
        return jnp.broadcast_to(flags.astype(F32)[:, None], (blocks, LANES))

    forward = (
        mirrored,
        gain.reshape(-1, poles).astype(BF16),
        mask_of(causal, ids == before[:blocks, None]),
        leave,
        (ids == lasts[:, None]).astype(F32),
        across,
        spread(before[:blocks] == lasts),
    )
    backward = (
        response,
        gain_rev.reshape(-1, poles).astype(BF16),
        mask_of(causal.T, ids == after[:, None]),
        leave_rev,
        (ids == firsts[:, None]).astype(F32),
        across,
        spread(after == firsts),
    )
    steps = jnp.arange(rows, dtype=F32)
    whole_leave = jnp.exp(-(rows - 1.0 - steps)[None, :] * rate.reshape(-1, 1))
    whole_leave = (whole_leave * (flat_ids == flat_ids[-1])[None, :]).astype(BF16)
    whole_leave_rev = jnp.exp(-steps[None, :] * rate.reshape(-1, 1))
    whole_leave_rev = (whole_leave_rev * (flat_ids == flat_ids[0])[None, :]).astype(BF16)

    def incoming(state, distance, alive):
        everything = lax.all_gather(state, "ctx").astype(F32)
        gap = jnp.maximum(distance, 0).astype(F32) * rows
        weight = jnp.exp(-gap[:, None, None] * rate_chan[None])
        kept = (alive & (distance >= 0))[:, None, None]
        return jnp.sum(jnp.where(kept, weight * everything, 0.0), axis=0)

    devices = jnp.arange(size, dtype=jnp.int32)
    skip = skip_gain[None, :]
    state = summarize(key_in, value_in, whole_leave, poles, members)
    enter = incoming(state, me - 1 - devices, ends == before[0])
    filtered, gated = run_conv(
        forward_kernel, (query_in, key_in, value_in), skip, forward, enter, (F32, BF16), poles, members
    )
    partial_value = lax.dot_general(
        gated, gathered, (((1,), (1,)), ((), ())), preferred_element_type=F32
    ).astype(BF16)
    mixed_out = lax.psum_scatter(partial_value, "grp", scatter_dimension=1, tiled=True)
    terms, finish = scatter_terms(grad_full, gated, size, me)
    terms, grad_full, gathered = lax.optimization_barrier((terms, grad_full, gathered))
    grad_proj = finish(terms)
    grad_gated = jnp.dot(grad_full, gathered, preferred_element_type=F32)
    state = summarize(grad_gated, query_in, whole_leave_rev, poles, members)
    leaving = incoming(state, devices - 1 - me, opens == after[-1])
    grad_query, grad_key, grad_value = run_conv(
        backward_kernel, (query_in, key_in, value_in, grad_gated, filtered), skip, backward,
        leaving, (BF16, BF16, BF16), poles, members
    )
    return (mixed_out, grad_query, grad_key, grad_value, grad_proj)


def solution(mesh):
    return jax.shard_map(
        local,
        mesh=mesh,
        in_specs=(
            P("ctx", "grp"),
            P("ctx", "grp"),
            P("ctx", "grp"),
            P("grp", None),
            P("grp", None),
            P("grp"),
            P("ctx", "grp"),
            P(),
            P("ctx", "grp"),
        ),
        out_specs=(
            P("ctx", "grp"),
            P("ctx", "grp"),
            P("ctx", "grp"),
            P("ctx", "grp"),
            P("ctx", "grp"),
        ),
        check_vma=False,
    )
```

time: 480 us -> 319 us (0.66)
  matrix products: 120 us -> 41.4 us
  local copies, waits for them, and re-layouts: 116 us -> 49.9 us
  Pallas kernels: 0 us -> 48.6 us
  waiting for transfers between devices: 142 us -> 96.7 us
  blocking collectives: 40 us -> 21 us
  starting transfers between devices: 0.15 us -> 15 us
  other arithmetic: 39.7 us -> 27.3 us
    dot_general x8 -> x9, matrix products: 105 us -> 30.2 us  [the longest x8 19.8 us: chunk(): lax.dot_general(part, gated, contract, preferred_element_type=F32)]
    reduce_scatter x2 -> x1, waiting for transfers between devices: 102 us -> 42.5 us  [local(): lax.psum_scatter(partial_value, 'grp', scatter_dimension=1, tiled=True)]
    gather x1 -> x0, local copies, waits for them, and re-layouts: 54.4 us -> none  [local(): toeplitz = jnp.take(lagged, lag_index, axis=1)]
    pallas_call x0 -> x4, Pallas kernels: none -> 48.6 us  [the longest x2 34.4 us: run_conv(): pl.pallas_call(functools.partial(kernel, count, poles, members, blocks),...]
    all_gather x1 -> x0, waiting for transfers between devices: 39.1 us -> none  [local(): gathered = lax.all_gather(out_proj, 'ctx', axis=0, tiled=True)]
    all_gather x1, waiting for transfers between devices: 0.01 us -> 34.8 us  [local(): grad_full = lax.all_gather(grad_out, 'grp', axis=1, tiled=True)]
    rev x0 -> x2, local copies, waits for them, and re-layouts: none -> 30.5 us  [the longest x1 30.4 us: local(): gain_rev = gain[:, ::-1, :]]
    all_gather x4 -> x2, blocking collectives: 40 us -> 21 us  [incoming(): everything = lax.all_gather(state, 'ctx').astype(F32)]
  transfers between devices with their start and end apart: 4 -> 21, of which waited for: 2 -> 4; matrix products, arithmetic and copies ran while one was open for 51% -> 37% of each run, Pallas kernels for 0% -> 15%
where the time goes in v1:
time: 319 us; the launch traced here: 314 us
  waiting for transfers between devices  96.7 us (30%)
  local copies, waits for them, and re-layouts  49.9 us (16%)
  Pallas kernels  48.6 us (15%)
  matrix products  41.4 us (13%)
  other arithmetic  27.3 us (9%)
  blocking collectives  21 us (7%)
  starting transfers between devices  15 us (5%)
  between operations  14.5 us (5%)
    reduce_scatter x1, waiting for transfers between devices, local(): lax.psum_scatter(partial_value, 'grp', scatter_dimension=1, tiled=True)  42.5 us
    all_gather x1, waiting for transfers between devices, local(): grad_full = lax.all_gather(grad_out, 'grp', axis=1, tiled=True)  34.8 us
    pallas_call x2, Pallas kernels, run_conv(): pl.pallas_call(functools.partial(kernel, count, poles, members, blocks),...  34.4 us
    rev x1, local copies, waits for them, and re-layouts, local(): gain_rev = gain[:, ::-1, :]  30.4 us
    all_gather x2, blocking collectives, incoming(): everything = lax.all_gather(state, 'ctx').astype(F32)  21 us
    dot_general x8, matrix products, chunk(): lax.dot_general(part, gated, contract, preferred_element_type=F32)  19.8 us
    ppermute x19, waiting for transfers between devices, swap(): return lax.ppermute(value, 'ctx', [(i, i ^ flip) for i in range(size)])  18.8 us
    ppermute x19, starting transfers between devices, swap(): return lax.ppermute(value, 'ctx', [(i, i ^ flip) for i in range(size)])  14.9 us
  transfers between devices with their start and end apart: 21, of which 4 were waited for; matrix products, arithmetic and copies ran while one was open for 37% of the time, Pallas kernels for 15%

profile of v1, /device:TPU:0, one launch (start us, length us, event | category | flops | bytes accessed | tf_op | source)
XLA Modules:
  0.0 314.4 jit_solution(17426615623257236144)
XLA Ops:
  8.0 3.0 collective-permute-start
  18.9 3.3 %multiply_convert_fusion = (bf16[1024,1024]{1,0:T(8,128)(2,1)}, bf16[1024,1024]{1,0:T(8,128)(2,1)}) fusion(f32[1024]{0:T(1024)S(1)} %get-tuple-element.49, f32[1024]{0:T(1024)S(1)} %get-tuple-element.71, f32[1024]{0:T(1024)S(1)} %mul.268, f32[1024]{0:T(1024)S(1)} %get-tuple-element.50, f32[1024]{0:T(1024)S(1)} %get-tuple-element.72), kind=kLoop, calls=%fused_computation.5 | loop fusion | flops 6291456 | bytes 4214784 | tf_op jit(solution)/shard_map/convert_element_type | solution.py:265
  22.2 7.0 %shard_map.128 = bf16[16,1024]{1,0:T(8,128)(2,1)} custom-call(bf16[1024,1024]{1,0:T(8,128)(2,1)} %key.3, bf16[1024,1024]{1,0:T(8,128)(2,1)} %value.3, bf16[1024,1024]{1,0:T(8,128)(2,1)} %get-tuple-element.48.leave_ref), custom_call_target="tpu_custom_call" | custom-call | flops 268435456 | bytes 8388608 | tf_op jit(solution)/shard_map/pallas_call | solution.py:37
  29.2 11.2 %all-gather = bf16[128,1024]{1,0:T(8,128)(2,1)S(1)} all-gather(bf16[16,1024]{1,0:T(8,128)(2,1)} %shard_map.128), channel_id=2, replica_groups=mesh['ctx'=8,'grp'=4] {'ctx'}, dimensions={0}, use_global_device_ids=true | all-gather | bytes 294912 | tf_op jit(solution)/shard_map/all_gather | solution.py:268
  50.7 16.9 %shard_map.129 = (f32[1024,1024]{1,0:T(8,128)}, bf16[1024,1024]{1,0:T(8,128)(2,1)}) custom-call(bf16[1024,1024]{1,0:T(8,128)(2,1)} %query.3, bf16[1024,1024]{1,0:T(8,128)(2,1)} %key.3, bf16[1024,1024]{1,0:T(8,128)(2,1)} %value.3, f32[1,1024]{1,0:T(1,128)} %bitcast.56, f32[64,128]{1,0:T(8,128)} %pad_maximum_fusion.1.lag, bf16[8192,16]{1,0:T(8,128)(2,1)} %fusion.2.gain, ...), custom_call_target="tpu_custom_call" | custom-call | flops 4294967296 | bytes 14680064 | tf_op jit(solution)/shard_map/pallas_call | solution.py:127
  77.6 3.2 %copy-done.2 = bf16[4096,1024]{1,0:T(8,128)(2,1)} copy-done((bf16[4096,1024]{1,0:T(8,128)(2,1)}, bf16[4096,1024]{1,0:T(8,128)(2,1)S(1)}, u32[]{:S(2)}) %copy-start.2) | copy-done | bytes 8388632
  80.8 11.2 %convolution_convert_fusion = bf16[1024,4096]{1,0:T(8,128)(2,1)} fusion(bf16[1024,1024]{1,0:T(8,128)(2,1)S(1)} %copy-done, bf16[4096,1024]{1,0:T(8,128)(2,1)S(1)} %constant_dynamic-update-slice_fusion), kind=kOutput, calls=%fused_computation | convolution fusion | flops 8594128896 | bytes 18874368 | tf_op jit(solution)/shard_map/dot_general | solution.py:281
  94.9 30.4 %rev.7 = bf16[64,128,16]{2,1,0:T(8,128)(2,1)} reverse(bf16[64,128,16]{2,1,0:T(8,128)(2,1)} %exponential_multiply_fusion), dimensions={1} | reverse | bytes 524288 | tf_op jit(solution)/shard_map/rev | solution.py:228
  127.2 34.8 %all-gather.4.cloned.1.call-done = bf16[1024,4096]{1,0:T(8,128)(2,1)} async-done(((bf16[1024,1024]{1,0:T(8,128)(2,1)}), bf16[1024,4096]{1,0:T(8,128)(2,1)}) %all-gather.4.cloned.1.call-update) | async-done | bytes 8388624 | tf_op jit(solution)/shard_map/all_gather | solution.py:211
  162.0 3.6 %convolution_convert_fusion.1 = bf16[512,1024]{1,0:T(8,128)(2,1)} fusion(bf16[1024,1024]{1,0:T(8,128)(2,1)S(1)} %copy-done, bf16[1024,4096]{1,0:T(8,128)(2,1)} %all-gather.4.cloned.1.call-done, s32[]{:T(128)S(6)} %select_n.54), kind=kOutput, calls=%fused_computation.13 | convolution fusion | flops 1074266112 | bytes 4194308 | tf_op jit(solution)/shard_map/dot_general | solution.py:182
  165.6 2.5 convolution_convert_fusion.2
  168.1 2.3 convolution_convert_fusion.3
  170.4 2.3 convolution_convert_fusion.4
  172.7 2.3 convolution_convert_fusion.5
  174.9 2.3 convolution_convert_fusion.6
  177.2 2.3 convolution_convert_fusion.7
  179.5 2.3 convolution_convert_fusion.8
  182.8 10.4 %fusion.32.a_ref.grad_gated = f32[1024,1024]{1,0:T(8,128)} fusion(bf16[1024,4096]{1,0:T(8,128)(2,1)S(1)} %copy-done.1, bf16[4096,1024]{1,0:T(8,128)(2,1)S(1)} %bitcast.52), kind=kOutput, calls=%fused_computation.118 | convolution fusion | flops 8589934592 | bytes 20971520 | tf_op jit(solution)/shard_map/dot_general | solution.py:288
  193.2 7.2 %shard_map.130 = bf16[16,1024]{1,0:T(8,128)(2,1)} custom-call(f32[1024,1024]{1,0:T(8,128)} %fusion.32.a_ref.grad_gated, bf16[1024,1024]{1,0:T(8,128)(2,1)} %query.3, bf16[1024,1024]{1,0:T(8,128)(2,1)} %get-tuple-element.47.leave_ref), custom_call_target="tpu_custom_call" | custom-call | flops 268435456 | bytes 8388608 | tf_op jit(solution)/shard_map/pallas_call | solution.py:37
  200.4 9.9 %all-gather.1 = bf16[128,1024]{1,0:T(8,128)(2,1)S(1)} all-gather(bf16[16,1024]{1,0:T(8,128)(2,1)} %shard_map.130), channel_id=3, replica_groups=mesh['ctx'=8,'grp'=4] {'ctx'}, dimensions={0}, use_global_device_ids=true | all-gather | bytes 294912 | tf_op jit(solution)/shard_map/all_gather | solution.py:268
  220.6 5.8 %collective-permute-done.17 = bf16[512,512]{1,0:T(8,128)(2,1)S(1)} collective-permute-done((bf16[512,512]{1,0:T(8,128)(2,1)S(1)}, bf16[512,512]{1,0:T(8,128)(2,1)S(1)}, u32[]{:S(2)}, u32[]{:S(2)}) %collective-permute-start.17) | collective-permute-done | bytes 524320 | tf_op jit(solution)/shard_map/ppermute | solution.py:151
  228.7 12.9 %collective-permute-done.14 = bf16[512,512]{1,0:T(8,128)(2,1)S(1)} collective-permute-done((bf16[512,512]{1,0:T(8,128)(2,1)S(1)}, bf16[512,512]{1,0:T(8,128)(2,1)S(1)}, u32[]{:S(2)}, u32[]{:S(2)}) %collective-permute-start.14) | collective-permute-done | bytes 524320 | tf_op jit(solution)/shard_map/ppermute | solution.py:151
  244.0 17.5 %shard_map.131 = (bf16[1024,1024]{1,0:T(8,128)(2,1)}, bf16[1024,1024]{1,0:T(8,128)(2,1)}, bf16[1024,1024]{1,0:T(8,128)(2,1)}) custom-call(bf16[1024,1024]{1,0:T(8,128)(2,1)} %query.3, bf16[1024,1024]{1,0:T(8,128)(2,1)} %key.3, bf16[1024,1024]{1,0:T(8,128)(2,1)} %value.3, f32[1024,1024]{1,0:T(8,128)} %fusion.32.a_ref.grad_gated, ...), custom_call_target="tpu_custom_call" | custom-call | flops 4294967296 | bytes 14680064 | tf_op jit(solution)/shard_map/pallas_call | solution.py:127
  265.1 42.5 %reduce-scatter.2.cloned.1.call-done = bf16[1024,1024]{1,0:T(8,128)(2,1)} async-done(((bf16[1024,4096]{1,0:T(8,128)(2,1)}), bf16[1024,1024]{1,0:T(8,128)(2,1)}) %reduce-scatter.2.cloned.1.call-update) | async-done | bytes 2097168 | tf_op jit(solution)/shard_map/reduce_scatter | solution.py:284
  (137 shorter events, 52.9 us)
Async XLA Ops:
  7.2 154.8 %all-gather.4.cloned.1.call-start = ((), (), s32[]{:S(2)}) async-start(), calls=%async_computation.2 | async-start | bytes 10485760 | tf_op jit(solution)/shard_map/all_gather | solution.py:211
  7.9 299.7 %reduce-scatter.2.cloned.1.call-start = ((), (), s32[]{:S(2)}) async-start(), calls=%async_computation.1 | async-start | bytes 10485760 | tf_op jit(solution)/shard_map/reduce_scatter | solution.py:284
  8.0 38.3 %collective-permute-start = (bf16[512,1024]{1,0:T(8,128)(2,1)}, bf16[512,1024]{1,0:T(8,128)(2,1)}, u32[]{:S(2)}, u32[]{:S(2)}) collective-permute-start(bf16[512,1024]{1,0:T(8,128)(2,1)} %param.15), channel_id=1, source_target_pairs={{0,8},{4,12},{8,0},{12,4},{16,24},{20,28},{24,16},{28,20},{1,9},{5... | collective-permute-start | bytes 3145736 | tf_op jit(solution)/shard_map/ppermute | solution.py:151
  11.0 37.0 %collective-permute-start.1 = (bf16[512,1024]{1,0:T(8,128)(2,1)}, bf16[512,1024]{1,0:T(8,128)(2,1)S(1)}, u32[]{:S(2)}, u32[]{:S(2)}) collective-permute-start(bf16[512,1024]{1,0:T(8,128)(2,1)} %param.15), channel_id=1, source_target_pairs={{0,16},{4,20},{8,24},{12,28},{16,0},{20,4},{24,8},{28,12},{1,17},{... | collective-permute-start | bytes 3145736 | tf_op jit(solution)/shard_map/ppermute | solution.py:151
  12.5 60.8 %collective-permute-start.4 = (bf16[512,1024]{1,0:T(8,128)(2,1)}, bf16[512,1024]{1,0:T(8,128)(2,1)}, u32[]{:S(2)}, u32[]{:S(2)}) collective-permute-start(bf16[512,1024]{1,0:T(8,128)(2,1)} %param.15), channel_id=1, source_target_pairs={{0,4},{4,0},{8,12},{12,8},{16,20},{20,16},{24,28},{28,24},{1,5},{5... | collective-permute-start | bytes 3145736 | tf_op jit(solution)/shard_map/ppermute | solution.py:151
  14.3 26.3 %copy-start.7 = (f32[64,128]{1,0:T(8,128)}, f32[64,128]{1,0:T(8,128)S(1)}, u32[]{:S(2)}) copy-start(f32[64,128]{1,0:T(8,128)S(1)} %multiply_reduce_fusion.lag) | copy-start | bytes 98308
  47.3 23.1 %collective-permute-start.2 = (bf16[256,1024]{1,0:T(8,128)(2,1)S(1)}, bf16[256,1024]{1,0:T(8,128)(2,1)}, u32[]{:S(2)}, u32[]{:S(2)}) collective-permute-start(bf16[256,1024]{1,0:T(8,128)(2,1)S(1)} %slice.83), channel_id=1, source_target_pairs={{0,16},{4,20},{8,24},{12,28},{16,0},{20,4},{24,8},{28,12},{1,17},{... | collective-permute-start | bytes 1572872 | tf_op jit(solution)/shard_map/ppermute | solution.py:151
  48.0 22.6 %collective-permute-start.3 = (bf16[256,1024]{1,0:T(8,128)(2,1)S(1)}, bf16[256,1024]{1,0:T(8,128)(2,1)}, u32[]{:S(2)}, u32[]{:S(2)}) collective-permute-start(bf16[256,1024]{1,0:T(8,128)(2,1)S(1)} %slice.84), channel_id=1, source_target_pairs={{0,8},{4,12},{8,0},{12,4},{16,24},{20,28},{24,16},{28,20},{1,9},{5... | collective-permute-start | bytes 1572872 | tf_op jit(solution)/shard_map/ppermute | solution.py:151
  49.5 25.2 %collective-permute-start.5 = (bf16[512,1024]{1,0:T(8,128)(2,1)}, bf16[512,1024]{1,0:T(8,128)(2,1)}, u32[]{:S(2)}, u32[]{:S(2)}) collective-permute-start(bf16[512,1024]{1,0:T(8,128)(2,1)} %collective-permute-done), channel_id=1, source_target_pairs={{0,4},{4,0},{8,12},{12,8},{16,20},{20,16},{24,28},{28,24},{1,5},{5... | collective-permute-start | bytes 3145736 | tf_op jit(solution)/shard_map/ppermute | solution.py:151
  49.5 26.6 %collective-permute-start.6 = (bf16[512,1024]{1,0:T(8,128)(2,1)S(1)}, bf16[512,1024]{1,0:T(8,128)(2,1)}, u32[]{:S(2)}, u32[]{:S(2)}) collective-permute-start(bf16[512,1024]{1,0:T(8,128)(2,1)S(1)} %collective-permute-done.1), channel_id=1, source_target_pairs={{0,4},{4,0},{8,12},{12,8},{16,20},{20,16},{24,28},{28,24},{1,5},{5... | collective-permute-start | bytes 3145736 | tf_op jit(solution)/shard_map/ppermute | solution.py:151
  70.5 7.0 %collective-permute-start.7 = (bf16[256,1024]{1,0:T(8,128)(2,1)}, bf16[256,1024]{1,0:T(8,128)(2,1)S(1)}, u32[]{:S(2)}, u32[]{:S(2)}) collective-permute-start(bf16[256,1024]{1,0:T(8,128)(2,1)} %collective-permute-done.2), channel_id=1, source_target_pairs={{0,4},{4,0},{8,12},{12,8},{16,20},{20,16},{24,28},{28,24},{1,5},{5... | collective-permute-start | bytes 1572872 | tf_op jit(solution)/shard_map/ppermute | solution.py:151
  70.6 7.0 %collective-permute-start.8 = (bf16[256,1024]{1,0:T(8,128)(2,1)}, bf16[256,1024]{1,0:T(8,128)(2,1)S(1)}, u32[]{:S(2)}, u32[]{:S(2)}) collective-permute-start(bf16[256,1024]{1,0:T(8,128)(2,1)} %collective-permute-done.3), channel_id=1, source_target_pairs={{0,4},{4,0},{8,12},{12,8},{16,20},{20,16},{24,28},{28,24},{1,5},{5... | collective-permute-start | bytes 1572872 | tf_op jit(solution)/shard_map/ppermute | solution.py:151
  181.8 31.1 %collective-permute-start.10 = (bf16[512,1024]{1,0:T(8,128)(2,1)}, bf16[512,1024]{1,0:T(8,128)(2,1)}, u32[]{:S(2)}, u32[]{:S(2)}) collective-permute-start(bf16[512,1024]{1,0:T(8,128)(2,1)} %convolution_convert_fusion.5), channel_id=1, source_target_pairs={{0,4},{4,0},{8,12},{12,8},{16,20},{20,16},{24,28},{28,24},{1,5},{5... | collective-permute-start | bytes 3145736 | tf_op jit(solution)/shard_map/ppermute | solution.py:151
  181.9 29.2 %collective-permute-start.13 = (bf16[512,1024]{1,0:T(8,128)(2,1)}, bf16[512,1024]{1,0:T(8,128)(2,1)S(1)}, u32[]{:S(2)}, u32[]{:S(2)}) collective-permute-start(bf16[512,1024]{1,0:T(8,128)(2,1)} %convolution_convert_fusion.1), channel_id=1, source_target_pairs={{0,4},{4,0},{8,12},{12,8},{16,20},{20,16},{24,28},{28,24},{1,5},{5... | collective-permute-start | bytes 3145736 | tf_op jit(solution)/shard_map/ppermute | solution.py:151
  182.3 35.1 %collective-permute-start.12 = (bf16[512,1024]{1,0:T(8,128)(2,1)}, bf16[512,1024]{1,0:T(8,128)(2,1)}, u32[]{:S(2)}, u32[]{:S(2)}) collective-permute-start(bf16[512,1024]{1,0:T(8,128)(2,1)} %convolution_convert_fusion.3), channel_id=1, source_target_pairs={{0,4},{4,0},{8,12},{12,8},{16,20},{20,16},{24,28},{28,24},{1,5},{5... | collective-permute-start | bytes 3145736 | tf_op jit(solution)/shard_map/ppermute | solution.py:151
  182.4 79.1 %collective-permute-start.9 = (bf16[512,1024]{1,0:T(8,128)(2,1)}, bf16[512,1024]{1,0:T(8,128)(2,1)}, u32[]{:S(2)}, u32[]{:S(2)}) collective-permute-start(bf16[512,1024]{1,0:T(8,128)(2,1)} %convolution_convert_fusion.7), channel_id=1, source_target_pairs={{0,4},{4,0},{8,12},{12,8},{16,20},{20,16},{24,28},{28,24},{1,5},{5... | collective-permute-start | bytes 3145736 | tf_op jit(solution)/shard_map/ppermute | solution.py:151
  200.4 12.6 %copy-start.5 = (bf16[512,1024]{1,0:T(8,128)(2,1)S(1)}, bf16[512,1024]{1,0:T(8,128)(2,1)}, u32[]{:S(2)}) copy-start(bf16[512,1024]{1,0:T(8,128)(2,1)} %convolution_convert_fusion.6) | copy-start | bytes 3145732
  211.6 14.8 %collective-permute-start.17 = (bf16[512,512]{1,0:T(8,128)(2,1)S(1)}, bf16[512,512]{1,0:T(8,128)(2,1)S(1)}, u32[]{:S(2)}, u32[]{:S(2)}) collective-permute-start(bf16[512,512]{1,0:T(8,128)(2,1)S(1)} %get-tuple-element.43), channel_id=1, source_target_pairs={{0,16},{4,20},{8,24},{12,28},{16,0},{20,4},{24,8},{28,12},{1,17},{... | collective-permute-start | bytes 1572872 | tf_op jit(solution)/shard_map/ppermute | solution.py:151
  215.4 47.7 %collective-permute-start.11 = (bf16[512,512]{1,0:T(8,128)(2,1)}, bf16[512,512]{1,0:T(8,128)(2,1)S(1)}, u32[]{:S(2)}, u32[]{:S(2)}) collective-permute-start(bf16[512,512]{1,0:T(8,128)(2,1)} %slice.112), channel_id=1, source_target_pairs={{0,8},{4,12},{8,0},{12,4},{16,24},{20,28},{24,16},{28,20},{1,9},{5... | collective-permute-start | bytes 1572872 | tf_op jit(solution)/shard_map/ppermute | solution.py:151
  216.1 25.5 %collective-permute-start.14 = (bf16[512,512]{1,0:T(8,128)(2,1)S(1)}, bf16[512,512]{1,0:T(8,128)(2,1)S(1)}, u32[]{:S(2)}, u32[]{:S(2)}) collective-permute-start(bf16[512,512]{1,0:T(8,128)(2,1)S(1)} %get-tuple-element.42), channel_id=1, source_target_pairs={{0,8},{4,12},{8,0},{12,4},{16,24},{20,28},{24,16},{28,20},{1,9},{5... | collective-permute-start | bytes 1572872 | tf_op jit(solution)/shard_map/ppermute | solution.py:151
  219.9 43.2 %collective-permute-start.16 = (bf16[512,512]{1,0:T(8,128)(2,1)}, bf16[512,512]{1,0:T(8,128)(2,1)S(1)}, u32[]{:S(2)}, u32[]{:S(2)}) collective-permute-start(bf16[512,512]{1,0:T(8,128)(2,1)} %slice.111), channel_id=1, source_target_pairs={{0,16},{4,20},{8,24},{12,28},{16,0},{20,4},{24,8},{28,12},{1,17},{... | collective-permute-start | bytes 1572872 | tf_op jit(solution)/shard_map/ppermute | solution.py:151
  227.4 35.7 %collective-permute-start.18 = (bf16[512,512]{1,0:T(8,128)(2,1)}, bf16[512,512]{1,0:T(8,128)(2,1)S(1)}, u32[]{:S(2)}, u32[]{:S(2)}) collective-permute-start(bf16[512,512]{1,0:T(8,128)(2,1)} %fusion.3), channel_id=1, source_target_pairs={{0,8},{4,12},{8,0},{12,4},{16,24},{20,28},{24,16},{28,20},{1,9},{5... | collective-permute-start | bytes 1572872 | tf_op jit(solution)/shard_map/ppermute | solution.py:151
  242.6 20.6 %collective-permute-start.15 = (bf16[512,512]{1,0:T(8,128)(2,1)}, bf16[512,512]{1,0:T(8,128)(2,1)S(1)}, u32[]{:S(2)}, u32[]{:S(2)}) collective-permute-start(bf16[512,512]{1,0:T(8,128)(2,1)} %fusion.5), channel_id=1, source_target_pairs={{0,16},{4,20},{8,24},{12,28},{16,0},{20,4},{24,8},{28,12},{1,17},{... | collective-permute-start | bytes 1572872 | tf_op jit(solution)/shard_map/ppermute | solution.py:151
  244.0 17.5 %copy-start.3 = (bf16[512,1024]{1,0:T(8,128)(2,1)S(1)}, bf16[512,1024]{1,0:T(8,128)(2,1)}, u32[]{:S(2)}) copy-start(bf16[512,1024]{1,0:T(8,128)(2,1)} %convolution_convert_fusion.8) | copy-start | bytes 3145732
  (8 other events, 49.5 us)
Sparse Core Ops, SparseCore 0:
  9.6 152.3 all-gather.3
  164.9 142.6 reduce-scatter.1

commit v2 on v1

--- a/solution.py
+++ b/solution.py
@@ -170,6 +170,37 @@
     return whole
 
 
+def after(value, *others):
+    return lax.optimization_barrier((value, others))[0]
+
+
+def scatter_columns(value, axis, before_last):
+    size, me = lax.axis_size(axis), lax.axis_index(axis)
+    width = value.shape[1] // size
+
+    def own(position):
+        start = jnp.clip(position, 0, size - 1) * width
+        return lax.dynamic_slice_in_dim(value, start, width, axis=1).astype(F32)
+
+    right = left = None
+    for step in range(1, size):
+        up, down = own(me + size - step), own(me - size + step)
+        if step == size - 1:
+            right, left = after((right, left), before_last)
+        if right is not None:
+            up, down = up + right.astype(F32), down + left.astype(F32)
+        right = lax.ppermute(up.astype(BF16), axis, [(z, z + 1) for z in range(step)])
+        left = lax.ppermute(
+            down.astype(BF16), axis, [(size - 1 - z, size - 2 - z) for z in range(step)]
+        )
+
+    def finish(*others):
+        last_right, last_left = after((right, left), others)
+        return (own(me) + last_right.astype(F32) + last_left.astype(F32)).astype(BF16)
+
+    return finish
+
+
 def scatter_terms(grad_full, gated, size, me):
     contract = (((0,), (0,)), ((), ()))
     if size != 8:
@@ -181,13 +212,14 @@
         part = lax.dynamic_slice_in_dim(grad_full, (me ^ flip) * width, width, axis=1)
         return lax.dot_general(part, gated, contract, preferred_element_type=F32).astype(BF16)
 
-    terms = {flip: chunk(flip) for flip in (7, 3, 5, 1, 6, 2, 4, 0)}
+    arriving = {flip: swap(chunk(flip ^ 1), 1, size) for flip in (6, 2, 4, 0)}
+    terms = {flip: chunk(flip) for flip in (6, 2, 4, 0)}
 
     def finish(terms):
         half = gated.shape[1] // 2
         sums = {}
         for flip in (6, 2, 4, 0):
-            sums[flip] = terms[flip].astype(F32) + swap(terms[flip ^ 1], 1, size).astype(F32)
+            sums[flip] = terms[flip].astype(F32) + arriving[flip].astype(F32)
 
         def route(columns, near, far):
             far_sum = sums[far][:, columns] + swap(sums[6][:, columns].astype(BF16), near, size).astype(F32)
@@ -215,7 +247,7 @@
     ids = flat_ids.reshape(blocks, BLOCK)
     firsts, lasts = ids[:, 0], ids[:, -1]
     before = doc_index(starts, me * rows - 1 + BLOCK * jnp.arange(blocks + 1, dtype=jnp.int32))
-    after = doc_index(starts, me * rows + BLOCK * jnp.arange(1, blocks + 1, dtype=jnp.int32))
+    following = doc_index(starts, me * rows + BLOCK * jnp.arange(1, blocks + 1, dtype=jnp.int32))
     ends = doc_index(starts, rows * jnp.arange(1, size + 1, dtype=jnp.int32) - 1)
     opens = doc_index(starts, rows * jnp.arange(size, dtype=jnp.int32))
     rate = 1.0 / decay_time
@@ -225,7 +257,7 @@
     response = jnp.sum(beta[:, :, None] * jnp.exp(-lags[None, None, :] * rate[:, :, None]), axis=1)
     mirrored = jnp.concatenate([response[:, :1], response[:, :0:-1]], axis=1)
     gain = beta[:, None, :] * jnp.exp(-(lags + 1.0)[None, :, None] * rate[:, None, :])
-    gain_rev = gain[:, ::-1, :]
+    gain_rev = beta[:, None, :] * jnp.exp(-(BLOCK - lags)[None, :, None] * rate[:, None, :])
     leave_rev = jnp.exp(-lags[None, :] * rate.reshape(-1, 1))
     leave = jnp.exp(-(BLOCK - 1.0 - lags)[None, :] * rate.reshape(-1, 1))
     across = jnp.exp(-BLOCK * rate_chan)
@@ -252,11 +284,11 @@
     backward = (
         response,
         gain_rev.reshape(-1, poles).astype(BF16),
-        mask_of(causal.T, ids == after[:, None]),
+        mask_of(causal.T, ids == following[:, None]),
         leave_rev,
         (ids == firsts[:, None]).astype(F32),
         across,
-        spread(after == firsts),
+        spread(following == firsts),
     )
     steps = jnp.arange(rows, dtype=F32)
     whole_leave = jnp.exp(-(rows - 1.0 - steps)[None, :] * rate.reshape(-1, 1))
@@ -281,17 +313,18 @@
     partial_value = lax.dot_general(
         gated, gathered, (((1,), (1,)), ((), ())), preferred_element_type=F32
     ).astype(BF16)
-    mixed_out = lax.psum_scatter(partial_value, "grp", scatter_dimension=1, tiled=True)
     terms, finish = scatter_terms(grad_full, gated, size, me)
+    finish_mixed = scatter_columns(partial_value, "grp", terms)
     terms, grad_full, gathered = lax.optimization_barrier((terms, grad_full, gathered))
     grad_proj = finish(terms)
     grad_gated = jnp.dot(grad_full, gathered, preferred_element_type=F32)
     state = summarize(grad_gated, query_in, whole_leave_rev, poles, members)
-    leaving = incoming(state, devices - 1 - me, opens == after[-1])
+    leaving = incoming(state, devices - 1 - me, opens == following[-1])
     grad_query, grad_key, grad_value = run_conv(
         backward_kernel, (query_in, key_in, value_in, grad_gated, filtered), skip, backward,
         leaving, (BF16, BF16, BF16), poles, members
     )
+    mixed_out = finish_mixed(grad_query)
     return (mixed_out, grad_query, grad_key, grad_value, grad_proj)
 
 

time: 319 us -> 361 us (1.13)
  waiting for transfers between devices: 96.7 us -> 123 us
  local copies, waits for them, and re-layouts: 49.9 us -> 24 us
  starting transfers between devices: 15 us -> 38.1 us
  other arithmetic: 27.3 us -> 49.3 us
    ppermute x0 -> x6, waiting for transfers between devices: none -> 113 us  [the longest x3 108 us: scatter_columns(): lax.ppermute(up.astype(BF16), axis, [(z, z + 1) for z in range(step)])]
    reduce_scatter x1 -> x0, waiting for transfers between devices: 42.5 us -> none  [local(): lax.psum_scatter(partial_value, 'grp', scatter_dimension=1, tiled=True)]
    all_gather x1, waiting for transfers between devices: 34.8 us -> 0.01 us  [local(): grad_full = lax.all_gather(grad_out, 'grp', axis=1, tiled=True)]
    rev x1 -> x0, local copies, waits for them, and re-layouts: 30.4 us -> none  [local(): gain_rev = gain[:, ::-1, :]]
    ppermute x0 -> x6, starting transfers between devices: none -> 23.8 us  [the longest x3 18.6 us: scatter_columns(): lax.ppermute(up.astype(BF16), axis, [(z, z + 1) for z in range(step)])]
    convert_element_type x1 -> x4, other arithmetic: 2.23 us -> 22.9 us  [the longest x2 14 us: scatter_columns(): down.astype(BF16)]
    ppermute x19, waiting for transfers between devices: 18.8 us -> 9.32 us  [swap(): return lax.ppermute(value, 'ctx', [(i, i ^ flip) for i in range(size)])]
  transfers between devices with their start and end apart: 21 -> 26, of which waited for: 4 -> 5; matrix products, arithmetic and copies ran while one was open for 37% -> 28% of each run, Pallas kernels for 15% -> 14%
where the time goes in v2:
time: 361 us; the launch traced here: 357 us
  waiting for transfers between devices  123 us (34%)
  other arithmetic  49.3 us (14%)
  Pallas kernels  48.4 us (13%)
  matrix products  41.5 us (11%)
  starting transfers between devices  38.1 us (11%)
  local copies, waits for them, and re-layouts  24 us (7%)
  blocking collectives  17.9 us (5%)
  between operations  15 us (4%)
    ppermute x3, waiting for transfers between devices, scatter_columns(): lax.ppermute(up.astype(BF16), axis, [(z, z + 1) for z in range(step)])  108 us
    pallas_call x2, Pallas kernels, run_conv(): pl.pallas_call(functools.partial(kernel, count, poles, members, blocks),...  34.3 us
    dot_general x8, matrix products, chunk(): lax.dot_general(part, gated, contract, preferred_element_type=F32)  19.8 us
    ppermute x3, starting transfers between devices, scatter_columns(): lax.ppermute(up.astype(BF16), axis, [(z, z + 1) for z in range(step)])  18.6 us
    all_gather x2, blocking collectives, incoming(): everything = lax.all_gather(state, 'ctx').astype(F32)  17.9 us
    ppermute x19, starting transfers between devices, swap(): return lax.ppermute(value, 'ctx', [(i, i ^ flip) for i in range(size)])  14.3 us
    pallas_call x2, Pallas kernels, summarize(): pl.pallas_call(functools.partial(summary_kernel, count, poles, members),...  14.1 us
    convert_element_type x2, other arithmetic, scatter_columns(): down.astype(BF16)  14 us
  transfers between devices with their start and end apart: 26, of which 5 were waited for; matrix products, arithmetic and copies ran while one was open for 28% of the time, Pallas kernels for 14%

profile of v2, /device:TPU:0, one launch (start us, length us, event | category | flops | bytes accessed | tf_op | source)
XLA Modules:
  0.0 357.0 jit_solution(16984106267271918304)
XLA Ops:
  7.9 3.0 collective-permute-start
  15.3 3.8 %fusion.1 = (bf16[8192,16]{1,0:T(8,128)(2,1)}, bf16[8192,16]{1,0:T(8,128)(2,1)}) fusion(f32[8192]{0:T(1024)S(1)} %get-tuple-element.73, f32[64,16]{1,0:T(8,128)S(1)} %copy.26, f32[64,16]{1,0:T(8,128)S(1)} %copy.25, f32[8192]{0:T(1024)S(1)} %get-tuple-element.74), kind=kLoop, calls=%fused_computation.6 | loop fusion | flops 786432 | bytes 598016 | tf_op jit(solution)/shard_map/convert_element_type | solution.py:286
  21.1 3.3 multiply_convert_fusion
  24.4 6.9 %shard_map.128 = bf16[16,1024]{1,0:T(8,128)(2,1)} custom-call(bf16[1024,1024]{1,0:T(8,128)(2,1)} %key.3, bf16[1024,1024]{1,0:T(8,128)(2,1)} %value.3, bf16[1024,1024]{1,0:T(8,128)(2,1)} %get-tuple-element.56.leave_ref), custom_call_target="tpu_custom_call" | custom-call | flops 268435456 | bytes 8388608 | tf_op jit(solution)/shard_map/pallas_call | solution.py:37
  31.3 9.0 %all-gather = bf16[128,1024]{1,0:T(8,128)(2,1)S(1)} all-gather(bf16[16,1024]{1,0:T(8,128)(2,1)} %shard_map.128), channel_id=2, replica_groups=mesh['ctx'=8,'grp'=4] {'ctx'}, dimensions={0}, use_global_device_ids=true | all-gather | bytes 294912 | tf_op jit(solution)/shard_map/all_gather | solution.py:300
  50.7 16.9 %shard_map.129 = (f32[1024,1024]{1,0:T(8,128)}, bf16[1024,1024]{1,0:T(8,128)(2,1)}) custom-call(bf16[1024,1024]{1,0:T(8,128)(2,1)} %query.3, bf16[1024,1024]{1,0:T(8,128)(2,1)} %key.3, bf16[1024,1024]{1,0:T(8,128)(2,1)} %value.3, f32[1,1024]{1,0:T(1,128)} %bitcast.66, f32[64,128]{1,0:T(8,128)} %pad_maximum_fusion.1.lag, ...), custom_call_target="tpu_custom_call" | custom-call | flops 4294967296 | bytes 14680064 | tf_op jit(solution)/shard_map/pallas_call | solution.py:127
  77.6 3.3 copy-done.3
  80.9 11.3 %convolution_convert_fusion = bf16[1024,4096]{1,0:T(8,128)(2,1)S(1)} fusion(bf16[1024,1024]{1,0:T(8,128)(2,1)S(1)} %copy-done, bf16[4096,1024]{1,0:T(8,128)(2,1)} %copy-done.3), kind=kOutput, calls=%fused_computation | convolution fusion | flops 8594128896 | bytes 18874368 | tf_op jit(solution)/shard_map/dot_general | solution.py:313
  92.2 2.9 constant_dynamic-slice_fusion
  98.7 5.0 %collective-permute-start.9 = (bf16[1024,1024]{1,0:T(8,128)(2,1)}, bf16[1024,1024]{1,0:T(8,128)(2,1)}, u32[]{:S(2)}, u32[]{:S(2)}) collective-permute-start(bf16[1024,1024]{1,0:T(8,128)(2,1)} %get-tuple-element.45), channel_id=1, source_target_pairs={{0,1},{4,5},{8,9},{12,13},{16,17},{20,21},{24,25},{28,29}} | collective-permute-start | bytes 6291464 | tf_op jit(solution)/shard_map/ppermute | solution.py:192
  106.3 86.8 %collective-permute-done.9 = bf16[1024,1024]{1,0:T(8,128)(2,1)} collective-permute-done((bf16[1024,1024]{1,0:T(8,128)(2,1)}, bf16[1024,1024]{1,0:T(8,128)(2,1)}, u32[]{:S(2)}, u32[]{:S(2)}) %collective-permute-start.9) | collective-permute-done | bytes 2097184 | tf_op jit(solution)/shard_map/ppermute | solution.py:192
  193.1 7.7 %add_convert_fusion.3 = (bf16[1024,1024]{1,0:T(8,128)(2,1)}, bf16[1024,1024]{1,0:T(8,128)(2,1)}) fusion(bf16[1024,1024]{1,0:T(8,128)(2,1)} %collective-permute-done.11, bf16[1024,4096]{1,0:T(8,128)(2,1)} %copy-done.1, s32[]{:T(128)S(6)} %select_n.81, bf16[1024,1024]{1,0:T(8,128)(2,1)} %collective-permute-done.9, s32[]{:T(128)S(6)} %select_n.79), kind=kLoop, calls=%fused_computation.13 | loop fusion | flops 8388608 | bytes 12582920 | tf_op jit(solution)/shard_map/convert_element_type | solution.py:194
  200.8 5.7 %collective-permute-start.10 = (bf16[1024,1024]{1,0:T(8,128)(2,1)}, bf16[1024,1024]{1,0:T(8,128)(2,1)}, u32[]{:S(2)}, u32[]{:S(2)}) collective-permute-start(bf16[1024,1024]{1,0:T(8,128)(2,1)} %get-tuple-element.43), channel_id=1, source_target_pairs={{0,1},{1,2},{4,5},{5,6},{8,9},{9,10},{12,13},{13,14},{16,17},{17,1... | collective-permute-start | bytes 6291464 | tf_op jit(solution)/shard_map/ppermute | solution.py:192
  211.1 3.5 convolution_convert_fusion.6
  228.8 21.0 %collective-permute-done.10 = bf16[1024,1024]{1,0:T(8,128)(2,1)} collective-permute-done((bf16[1024,1024]{1,0:T(8,128)(2,1)}, bf16[1024,1024]{1,0:T(8,128)(2,1)}, u32[]{:S(2)}, u32[]{:S(2)}) %collective-permute-start.10) | collective-permute-done | bytes 2097184 | tf_op jit(solution)/shard_map/ppermute | solution.py:192
  249.8 6.4 %add_convert_fusion.1 = (bf16[1024,1024]{1,0:T(8,128)(2,1)}, bf16[1024,1024]{1,0:T(8,128)(2,1)}) fusion(bf16[1024,1024]{1,0:T(8,128)(2,1)} %collective-permute-done.12, bf16[1024,4096]{1,0:T(8,128)(2,1)S(1)} %bitcast.60, s32[]{:T(128)S(6)} %select_n.83, bf16[1024,1024]{1,0:T(8,128)(2,1)} %collective-permute-done.10, s32[]{:T(128)S(6)} %select_n.78), kind=kLoop, calls=%fused_computation.11 | loop fusion | flops 8388608 | bytes 12582920 | tf_op jit(solution)/shard_map/convert_element_type | solution.py:194
  256.2 7.8 %collective-permute-start.13 = (bf16[1024,1024]{1,0:T(8,128)(2,1)}, bf16[1024,1024]{1,0:T(8,128)(2,1)}, u32[]{:S(2)}, u32[]{:S(2)}) collective-permute-start(bf16[1024,1024]{1,0:T(8,128)(2,1)} %get-tuple-element.41), channel_id=1, source_target_pairs={{0,1},{1,2},{2,3},{4,5},{5,6},{6,7},{8,9},{9,10},{10,11},{12,13},{... | collective-permute-start | bytes 6291464 | tf_op jit(solution)/shard_map/ppermute | solution.py:192
  264.0 10.4 %fusion.33.a_ref.grad_gated = f32[1024,1024]{1,0:T(8,128)} fusion(bf16[1024,4096]{1,0:T(8,128)(2,1)S(1)} %copy-done.2, bf16[4096,1024]{1,0:T(8,128)(2,1)S(1)} %bitcast.62), kind=kOutput, calls=%fused_computation.130 | convolution fusion | flops 8589934592 | bytes 20971520 | tf_op jit(solution)/shard_map/dot_general | solution.py:320
  274.5 7.2 %shard_map.130 = bf16[16,1024]{1,0:T(8,128)(2,1)} custom-call(f32[1024,1024]{1,0:T(8,128)} %fusion.33.a_ref.grad_gated, bf16[1024,1024]{1,0:T(8,128)(2,1)} %query.3, bf16[1024,1024]{1,0:T(8,128)(2,1)} %get-tuple-element.55.leave_ref), custom_call_target="tpu_custom_call" | custom-call | flops 268435456 | bytes 8388608 | tf_op jit(solution)/shard_map/pallas_call | solution.py:37
  281.6 8.9 %all-gather.1 = bf16[128,1024]{1,0:T(8,128)(2,1)S(1)} all-gather(bf16[16,1024]{1,0:T(8,128)(2,1)} %shard_map.130), channel_id=3, replica_groups=mesh['ctx'=8,'grp'=4] {'ctx'}, dimensions={0}, use_global_device_ids=true | all-gather | bytes 294912 | tf_op jit(solution)/shard_map/all_gather | solution.py:300
  301.4 7.2 %collective-permute-done.23 = bf16[512,512]{1,0:T(8,128)(2,1)S(1)} collective-permute-done((bf16[512,512]{1,0:T(8,128)(2,1)S(1)}, bf16[512,512]{1,0:T(8,128)(2,1)S(1)}, u32[]{:S(2)}, u32[]{:S(2)}) %collective-permute-start.23) | collective-permute-done | bytes 524320 | tf_op jit(solution)/shard_map/ppermute | solution.py:151
  317.2 17.4 %shard_map.131 = (bf16[1024,1024]{1,0:T(8,128)(2,1)}, bf16[1024,1024]{1,0:T(8,128)(2,1)}, bf16[1024,1024]{1,0:T(8,128)(2,1)}) custom-call(bf16[1024,1024]{1,0:T(8,128)(2,1)} %query.3, bf16[1024,1024]{1,0:T(8,128)(2,1)} %key.3, bf16[1024,1024]{1,0:T(8,128)(2,1)} %value.3, f32[1024,1024]{1,0:T(8,128)} %fusion.33.a_ref.grad_gated, ...), custom_call_target="tpu_custom_call" | custom-call | flops 4294967296 | bytes 14680064 | tf_op jit(solution)/shard_map/pallas_call | solution.py:127
  336.3 5.0 %collective-permute-done.14 = bf16[1024,1024]{1,0:T(8,128)(2,1)S(1)} collective-permute-done((bf16[1024,1024]{1,0:T(8,128)(2,1)}, bf16[1024,1024]{1,0:T(8,128)(2,1)S(1)}, u32[]{:S(2)}, u32[]{:S(2)}) %collective-permute-start.14) | collective-permute-done | bytes 2097184 | tf_op jit(solution)/shard_map/ppermute | solution.py:193
  344.8 5.0 %add_convert_fusion = bf16[1024,1024]{1,0:T(8,128)(2,1)} fusion(bf16[1024,1024]{1,0:T(8,128)(2,1)S(1)} %collective-permute-done.14, bf16[1024,1024]{1,0:T(8,128)(2,1)} %collective-permute-done.13, bf16[1024,4096]{1,0:T(8,128)(2,1)} %copy-done.1, s32[]{:T(128)S(6)} %select_n.77), kind=kLoop, calls=%fused_computation.9 | loop fusion | flops 6291456 | bytes 8388612 | tf_op jit(solution)/shard_map/convert_element_type | solution.py:199
  (156 shorter events, 76.5 us)
Async XLA Ops:
  7.2 201.3 %all-gather.4.cloned.1.call-start = ((), (), s32[]{:S(2)}) async-start(), calls=%async_computation | async-start | bytes 10485760 | tf_op jit(solution)/shard_map/all_gather | solution.py:243
  7.9 38.3 %collective-permute-start = (bf16[512,1024]{1,0:T(8,128)(2,1)}, bf16[512,1024]{1,0:T(8,128)(2,1)}, u32[]{:S(2)}, u32[]{:S(2)}) collective-permute-start(bf16[512,1024]{1,0:T(8,128)(2,1)} %param.15), channel_id=1, source_target_pairs={{0,8},{4,12},{8,0},{12,4},{16,24},{20,28},{24,16},{28,20},{1,9},{5... | collective-permute-start | bytes 3145736 | tf_op jit(solution)/shard_map/ppermute | solution.py:151
  10.9 37.4 %collective-permute-start.1 = (bf16[512,1024]{1,0:T(8,128)(2,1)}, bf16[512,1024]{1,0:T(8,128)(2,1)S(1)}, u32[]{:S(2)}, u32[]{:S(2)}) collective-permute-start(bf16[512,1024]{1,0:T(8,128)(2,1)} %param.15), channel_id=1, source_target_pairs={{0,16},{4,20},{8,24},{12,28},{16,0},{20,4},{24,8},{28,12},{1,17},{... | collective-permute-start | bytes 3145736 | tf_op jit(solution)/shard_map/ppermute | solution.py:151
  12.4 60.8 %collective-permute-start.4 = (bf16[512,1024]{1,0:T(8,128)(2,1)}, bf16[512,1024]{1,0:T(8,128)(2,1)}, u32[]{:S(2)}, u32[]{:S(2)}) collective-permute-start(bf16[512,1024]{1,0:T(8,128)(2,1)} %param.15), channel_id=1, source_target_pairs={{0,4},{4,0},{8,12},{12,8},{16,20},{20,16},{24,28},{28,24},{1,5},{5... | collective-permute-start | bytes 3145736 | tf_op jit(solution)/shard_map/ppermute | solution.py:151
  47.3 23.2 %collective-permute-start.2 = (bf16[256,1024]{1,0:T(8,128)(2,1)S(1)}, bf16[256,1024]{1,0:T(8,128)(2,1)}, u32[]{:S(2)}, u32[]{:S(2)}) collective-permute-start(bf16[256,1024]{1,0:T(8,128)(2,1)S(1)} %slice.83), channel_id=1, source_target_pairs={{0,16},{4,20},{8,24},{12,28},{16,0},{20,4},{24,8},{28,12},{1,17},{... | collective-permute-start | bytes 1572872 | tf_op jit(solution)/shard_map/ppermute | solution.py:151
  48.4 22.2 %collective-permute-start.3 = (bf16[256,1024]{1,0:T(8,128)(2,1)S(1)}, bf16[256,1024]{1,0:T(8,128)(2,1)}, u32[]{:S(2)}, u32[]{:S(2)}) collective-permute-start(bf16[256,1024]{1,0:T(8,128)(2,1)S(1)} %slice.84), channel_id=1, source_target_pairs={{0,8},{4,12},{8,0},{12,4},{16,24},{20,28},{24,16},{28,20},{1,9},{5... | collective-permute-start | bytes 1572872 | tf_op jit(solution)/shard_map/ppermute | solution.py:151
  49.5 25.2 %collective-permute-start.5 = (bf16[512,1024]{1,0:T(8,128)(2,1)}, bf16[512,1024]{1,0:T(8,128)(2,1)}, u32[]{:S(2)}, u32[]{:S(2)}) collective-permute-start(bf16[512,1024]{1,0:T(8,128)(2,1)} %collective-permute-done), channel_id=1, source_target_pairs={{0,4},{4,0},{8,12},{12,8},{16,20},{20,16},{24,28},{28,24},{1,5},{5... | collective-permute-start | bytes 3145736 | tf_op jit(solution)/shard_map/ppermute | solution.py:151
  49.5 26.6 %collective-permute-start.6 = (bf16[512,1024]{1,0:T(8,128)(2,1)S(1)}, bf16[512,1024]{1,0:T(8,128)(2,1)}, u32[]{:S(2)}, u32[]{:S(2)}) collective-permute-start(bf16[512,1024]{1,0:T(8,128)(2,1)S(1)} %collective-permute-done.1), channel_id=1, source_target_pairs={{0,4},{4,0},{8,12},{12,8},{16,20},{20,16},{24,28},{28,24},{1,5},{5... | collective-permute-start | bytes 3145736 | tf_op jit(solution)/shard_map/ppermute | solution.py:151
  96.7 9.6 %collective-permute-start.11 = (bf16[1024,1024]{1,0:T(8,128)(2,1)}, bf16[1024,1024]{1,0:T(8,128)(2,1)}, u32[]{:S(2)}, u32[]{:S(2)}) collective-permute-start(bf16[1024,1024]{1,0:T(8,128)(2,1)} %get-tuple-element.44), channel_id=1, source_target_pairs={{3,2},{7,6},{11,10},{15,14},{19,18},{23,22},{27,26},{31,30}} | collective-permute-start | bytes 6291464 | tf_op jit(solution)/shard_map/ppermute | solution.py:193
  98.7 94.4 %collective-permute-start.9 = (bf16[1024,1024]{1,0:T(8,128)(2,1)}, bf16[1024,1024]{1,0:T(8,128)(2,1)}, u32[]{:S(2)}, u32[]{:S(2)}) collective-permute-start(bf16[1024,1024]{1,0:T(8,128)(2,1)} %get-tuple-element.45), channel_id=1, source_target_pairs={{0,1},{4,5},{8,9},{12,13},{16,17},{20,21},{24,25},{28,29}} | collective-permute-start | bytes 6291464 | tf_op jit(solution)/shard_map/ppermute | solution.py:192
  200.8 49.0 %collective-permute-start.10 = (bf16[1024,1024]{1,0:T(8,128)(2,1)}, bf16[1024,1024]{1,0:T(8,128)(2,1)}, u32[]{:S(2)}, u32[]{:S(2)}) collective-permute-start(bf16[1024,1024]{1,0:T(8,128)(2,1)} %get-tuple-element.43), channel_id=1, source_target_pairs={{0,1},{1,2},{4,5},{5,6},{8,9},{9,10},{12,13},{13,14},{16,17},{17,1... | collective-permute-start | bytes 6291464 | tf_op jit(solution)/shard_map/ppermute | solution.py:192
  206.5 43.3 %collective-permute-start.12 = (bf16[1024,1024]{1,0:T(8,128)(2,1)}, bf16[1024,1024]{1,0:T(8,128)(2,1)}, u32[]{:S(2)}, u32[]{:S(2)}) collective-permute-start(bf16[1024,1024]{1,0:T(8,128)(2,1)} %get-tuple-element.42), channel_id=1, source_target_pairs={{3,2},{2,1},{7,6},{6,5},{11,10},{10,9},{15,14},{14,13},{19,18},{18... | collective-permute-start | bytes 6291464 | tf_op jit(solution)/shard_map/ppermute | solution.py:193
  221.5 69.9 %collective-permute-start.19 = (bf16[512,1024]{1,0:T(8,128)(2,1)}, bf16[512,1024]{1,0:T(8,128)(2,1)}, u32[]{:S(2)}, u32[]{:S(2)}) collective-permute-start(bf16[512,1024]{1,0:T(8,128)(2,1)} %convolution_convert_fusion.1), channel_id=1, source_target_pairs={{0,4},{4,0},{8,12},{12,8},{16,20},{20,16},{24,28},{28,24},{1,5},{5... | collective-permute-start | bytes 3145736 | tf_op jit(solution)/shard_map/ppermute | solution.py:151
  223.8 70.6 %collective-permute-start.16 = (bf16[512,1024]{1,0:T(8,128)(2,1)}, bf16[512,1024]{1,0:T(8,128)(2,1)}, u32[]{:S(2)}, u32[]{:S(2)}) collective-permute-start(bf16[512,1024]{1,0:T(8,128)(2,1)} %convolution_convert_fusion.3), channel_id=1, source_target_pairs={{0,4},{4,0},{8,12},{12,8},{16,20},{20,16},{24,28},{28,24},{1,5},{5... | collective-permute-start | bytes 3145736 | tf_op jit(solution)/shard_map/ppermute | solution.py:151
  226.5 71.5 %collective-permute-start.18 = (bf16[512,1024]{1,0:T(8,128)(2,1)}, bf16[512,1024]{1,0:T(8,128)(2,1)}, u32[]{:S(2)}, u32[]{:S(2)}) collective-permute-start(bf16[512,1024]{1,0:T(8,128)(2,1)} %convolution_convert_fusion.2), channel_id=1, source_target_pairs={{0,4},{4,0},{8,12},{12,8},{16,20},{20,16},{24,28},{28,24},{1,5},{5... | collective-permute-start | bytes 3145736 | tf_op jit(solution)/shard_map/ppermute | solution.py:151
  249.8 64.8 %collective-permute-start.15 = (bf16[512,1024]{1,0:T(8,128)(2,1)}, bf16[512,1024]{1,0:T(8,128)(2,1)}, u32[]{:S(2)}, u32[]{:S(2)}) collective-permute-start(bf16[512,1024]{1,0:T(8,128)(2,1)} %convolution_convert_fusion.4), channel_id=1, source_target_pairs={{0,4},{4,0},{8,12},{12,8},{16,20},{20,16},{24,28},{28,24},{1,5},{5... | collective-permute-start | bytes 3145736 | tf_op jit(solution)/shard_map/ppermute | solution.py:151
  256.2 59.6 %collective-permute-start.13 = (bf16[1024,1024]{1,0:T(8,128)(2,1)}, bf16[1024,1024]{1,0:T(8,128)(2,1)}, u32[]{:S(2)}, u32[]{:S(2)}) collective-permute-start(bf16[1024,1024]{1,0:T(8,128)(2,1)} %get-tuple-element.41), channel_id=1, source_target_pairs={{0,1},{1,2},{2,3},{4,5},{5,6},{6,7},{8,9},{9,10},{10,11},{12,13},{... | collective-permute-start | bytes 6291464 | tf_op jit(solution)/shard_map/ppermute | solution.py:192
  291.4 50.0 %collective-permute-start.14 = (bf16[1024,1024]{1,0:T(8,128)(2,1)}, bf16[1024,1024]{1,0:T(8,128)(2,1)S(1)}, u32[]{:S(2)}, u32[]{:S(2)}) collective-permute-start(bf16[1024,1024]{1,0:T(8,128)(2,1)} %get-tuple-element.40), channel_id=1, source_target_pairs={{3,2},{2,1},{1,0},{7,6},{6,5},{5,4},{11,10},{10,9},{9,8},{15,14},{... | collective-permute-start | bytes 6291464 | tf_op jit(solution)/shard_map/ppermute | solution.py:193
  294.4 14.2 %collective-permute-start.23 = (bf16[512,512]{1,0:T(8,128)(2,1)S(1)}, bf16[512,512]{1,0:T(8,128)(2,1)S(1)}, u32[]{:S(2)}, u32[]{:S(2)}) collective-permute-start(bf16[512,512]{1,0:T(8,128)(2,1)S(1)} %get-tuple-element.49), channel_id=1, source_target_pairs={{0,16},{4,20},{8,24},{12,28},{16,0},{20,4},{24,8},{28,12},{1,17},{... | collective-permute-start | bytes 1572872 | tf_op jit(solution)/shard_map/ppermute | solution.py:151
  298.0 14.8 %collective-permute-start.20 = (bf16[512,512]{1,0:T(8,128)(2,1)S(1)}, bf16[512,512]{1,0:T(8,128)(2,1)S(1)}, u32[]{:S(2)}, u32[]{:S(2)}) collective-permute-start(bf16[512,512]{1,0:T(8,128)(2,1)S(1)} %get-tuple-element.48), channel_id=1, source_target_pairs={{0,8},{4,12},{8,0},{12,4},{16,24},{20,28},{24,16},{28,20},{1,9},{5... | collective-permute-start | bytes 1572872 | tf_op jit(solution)/shard_map/ppermute | solution.py:151
  308.6 32.7 %collective-permute-start.17 = (bf16[512,512]{1,0:T(8,128)(2,1)}, bf16[512,512]{1,0:T(8,128)(2,1)}, u32[]{:S(2)}, u32[]{:S(2)}) collective-permute-start(bf16[512,512]{1,0:T(8,128)(2,1)} %slice.112), channel_id=1, source_target_pairs={{0,8},{4,12},{8,0},{12,4},{16,24},{20,28},{24,16},{28,20},{1,9},{5... | collective-permute-start | bytes 1572872 | tf_op jit(solution)/shard_map/ppermute | solution.py:151
  312.8 28.6 %collective-permute-start.22 = (bf16[512,512]{1,0:T(8,128)(2,1)}, bf16[512,512]{1,0:T(8,128)(2,1)}, u32[]{:S(2)}, u32[]{:S(2)}) collective-permute-start(bf16[512,512]{1,0:T(8,128)(2,1)} %slice.111), channel_id=1, source_target_pairs={{0,16},{4,20},{8,24},{12,28},{16,0},{20,4},{24,8},{28,12},{1,17},{... | collective-permute-start | bytes 1572872 | tf_op jit(solution)/shard_map/ppermute | solution.py:151
  314.6 26.8 %collective-permute-start.24 = (bf16[512,512]{1,0:T(8,128)(2,1)}, bf16[512,512]{1,0:T(8,128)(2,1)}, u32[]{:S(2)}, u32[]{:S(2)}) collective-permute-start(bf16[512,512]{1,0:T(8,128)(2,1)} %fusion.4), channel_id=1, source_target_pairs={{0,8},{4,12},{8,0},{12,4},{16,24},{20,28},{24,16},{28,20},{1,9},{5... | collective-permute-start | bytes 1572872 | tf_op jit(solution)/shard_map/ppermute | solution.py:151
  315.8 25.6 %collective-permute-start.21 = (bf16[512,512]{1,0:T(8,128)(2,1)}, bf16[512,512]{1,0:T(8,128)(2,1)}, u32[]{:S(2)}, u32[]{:S(2)}) collective-permute-start(bf16[512,512]{1,0:T(8,128)(2,1)} %fusion.6), channel_id=1, source_target_pairs={{0,16},{4,20},{8,24},{12,28},{16,0},{20,4},{24,8},{28,12},{1,17},{... | collective-permute-start | bytes 1572872 | tf_op jit(solution)/shard_map/ppermute | solution.py:151
  (16 other events, 240.5 us)
Sparse Core Ops, SparseCore 0:
  9.6 193.0 all-gather.3
